TPU v7x, 32 devices: a whole 2x2x4 slice. The times are simulated.
32 devices in a mesh: blk: 8 (over z, y), frames: 4 (over x, core).
Axes of the slice: x: 2, y: 2, z: 4, core: 2. Of those that a mesh axis runs over, the one named last changes fastest.
Arguments:
- coarse_query: bfloat16 [64, 16, 256], P('blk'), may hold values from -125 to 125
- coarse_feat: bfloat16 [16, 8160, 256], P('frames', 'blk'), may hold values from -61 to 61
- fine_query: bfloat16 [64, 128], P(('blk', 'frames')), may hold values from -175 to 175
- fine_tiles: bfloat16 [16, 512, 64, 128], P('frames', 'blk'), may hold values from -61 to 61
- track_pos: int32 [2, 16, 64], P(None, None, ('blk', 'frames')), may hold values from 0 to 959, as said below
- tile_list: int32 [16, 8, 4, 8], P('frames', 'blk'), may hold values from 0 to 63, as said below
- tile_valid: int32 [16, 8, 4, 8], P('frames', 'blk'), may hold values from 0 to 1, as said below
Outputs:
- coarse_pos: float32 [2, 16, 64], P(None, 'frames', 'blk')
- fine_offset: float32 [2, 16, 64], P(None, None, ('blk', 'frames'))
Inputs may be any that keep to these rules, and one draw needn't show every extreme that they name: `tile_list`: in each list the valid slots come first and name distinct tiles of the group's window; padded slots hold 63; in every frame and group some owner's list is full. `tile_valid`: each list has at least 4 valid slots. `track_pos`: rows lie below 544 and columns below 960.
All inputs are finite; a program needn't handle non-finite values.
Results may differ from a plain program's by a relative error of at most 0.0003.
Values may be sent and summed in bfloat16 or wider, within the bound.
No kernel may reach another device: no remote copies, remote signals or barrier semaphores. Data moves between devices by JAX's collectives and lax.ppermute only.
A program may use at most 192 MiB of HBM per device.

v0:
```python
import math

import jax
import jax.numpy as jnp
from jax import lax
from jax.sharding import PartitionSpec as P

GH = 68
GW = 120
TILE = 8


spread_cells = 32.0


def refine_frame(descriptors, tile_block, tile_ids, tile_live, track_row, track_col, base_cell):
    slot_count, cell_count, channels = tile_block.shape
    flat_tiles = tile_block.reshape(slot_count * cell_count, channels)
    scores = jnp.einsum(
        "nc,kc->nk", descriptors, flat_tiles, preferred_element_type=jnp.float32
    ) * (1.0 / math.sqrt(channels))
    global_cell = base_cell + tile_ids
    inner_cell = jnp.arange(cell_count, dtype=jnp.int32)
    cell_row = (global_cell // GW * TILE)[:, None] + (inner_cell // TILE)[None, :]
    cell_col = (global_cell % GW * TILE)[:, None] + (inner_cell % TILE)[None, :]
    cell_row = cell_row.reshape(-1).astype(jnp.float32)
    cell_col = cell_col.reshape(-1).astype(jnp.float32)
    distance = (cell_row[None, :] - track_row[:, None]) ** 2 + (
        cell_col[None, :] - track_col[:, None]
    ) ** 2
    scores = scores - distance * (0.5 / (spread_cells * spread_cells))
    live_cells = jnp.broadcast_to(tile_live[:, None] > 0, (slot_count, cell_count)).reshape(-1)
    scores = jnp.where(live_cells[None, :], scores, -1e30)
    highest = jnp.max(scores, axis=1, keepdims=True)
    weights = jnp.exp(scores - highest)
    totals = jnp.sum(weights, axis=1)
    mean_row = jnp.sum(weights * cell_row[None, :], axis=1) / totals
    mean_col = jnp.sum(weights * cell_col[None, :], axis=1) / totals
    return ((mean_row - track_row) / spread_cells, (mean_col - track_col) / spread_cells)


def coarse_finish(row_mean, col_mean):
    row_heads = jnp.mean(row_mean, axis=2)
    col_heads = jnp.mean(col_mean, axis=2)
    return jnp.stack(
        [(row_heads - (GH - 1) / 2.0) / (GH / 4.0), (col_heads - (GW - 1) / 2.0) / (GW / 4.0)]
    )


def body(coarse_query, coarse_feat, fine_query, fine_tiles, track_pos, tile_list, tile_valid):
    track_group, heads, channels = coarse_query.shape
    frames_here, region, _ = coarse_feat.shape
    scale = 1.0 / math.sqrt(channels)
    group_start = lax.axis_index("blk") * region
    local_cells = group_start + jnp.arange(region, dtype=jnp.int32)
    local_row = (local_cells // GW).astype(jnp.float32)
    local_col = (local_cells % GW).astype(jnp.float32)
    track_step = max(1, 2048 // heads)
    shard_piece = lax.all_gather(coarse_query, "blk", axis=0, tiled=True)
    length = shard_piece.shape[0]
    blocks = []
    for offset in range(0, length, track_step):
        query_rows = shard_piece[offset : offset + track_step].reshape(-1, channels)
        scores = (
            jnp.einsum("rc,fpc->frp", query_rows, coarse_feat, preferred_element_type=jnp.float32)
            * scale
        )
        block_max = jnp.max(scores, axis=2)
        weights = jnp.exp(scores - block_max[:, :, None])
        totals = jnp.sum(weights, axis=2)
        row_sums = jnp.sum(weights * local_row[None, None, :], axis=2)
        col_sums = jnp.sum(weights * local_col[None, None, :], axis=2)
        stacked = jnp.stack([block_max, totals, row_sums, col_sums])
        blocks.append(stacked.reshape(4, frames_here, -1, heads))
    stats = jnp.concatenate(blocks, axis=2)
    maxima_all, totals_all, rows_all, cols_all = (
        lax.all_to_all(stats[0][None], "blk", split_axis=2, concat_axis=0, tiled=True),
        lax.all_to_all(stats[1][None], "blk", split_axis=2, concat_axis=0, tiled=True),
        lax.all_to_all(stats[2][None], "blk", split_axis=2, concat_axis=0, tiled=True),
        lax.all_to_all(stats[3][None], "blk", split_axis=2, concat_axis=0, tiled=True),
    )
    overall = jnp.max(maxima_all, axis=0)
    retain = jnp.exp(maxima_all - overall[None])
    totals = jnp.sum(totals_all * retain, axis=0)
    row_mean = jnp.sum(rows_all * retain, axis=0) / totals
    col_mean = jnp.sum(cols_all * retain, axis=0) / totals
    coarse_pos = coarse_finish(row_mean, col_mean)
    list_ids = jnp.transpose(tile_list[:, 0], (1, 0, 2))
    list_live = jnp.transpose(tile_valid[:, 0], (1, 0, 2))
    picked = fine_tiles[jnp.arange(frames_here, dtype=jnp.int32)[None, :, None], list_ids]
    per_frame = jax.vmap(refine_frame, in_axes=(None, 0, 0, 0, 0, 0, None))
    got_tiles, got_ids, got_live = (
        lax.all_to_all(picked, "frames", split_axis=0, concat_axis=0, tiled=True),
        lax.all_to_all(list_ids, "frames", split_axis=0, concat_axis=0, tiled=True),
        lax.all_to_all(list_live, "frames", split_axis=0, concat_axis=0, tiled=True),
    )
    window = got_tiles.shape[0] * got_tiles.shape[1]
    got_tiles = got_tiles.reshape((window,) + got_tiles.shape[2:])
    got_ids = got_ids.reshape(window, -1)
    got_live = got_live.reshape(window, -1)
    places = track_pos.astype(jnp.float32)
    rows_out, cols_out = per_frame(
        fine_query, got_tiles, got_ids, got_live, places[0], places[1], group_start
    )
    fine_offset = jnp.stack([rows_out, cols_out])
    return (coarse_pos, fine_offset)


def solution(mesh):
    return jax.shard_map(
        body,
        mesh=mesh,
        in_specs=(
            P("blk", None, None),
            P("frames", "blk", None),
            P(("blk", "frames"), None),
            P("frames", "blk", None, None),
            P(None, None, ("blk", "frames")),
            P("frames", "blk", None, None),
            P("frames", "blk", None, None),
        ),
        out_specs=(P(None, "frames", "blk"), P(None, None, ("blk", "frames"))),
        check_vma=False,
    )
```

profile of v0, /device:TPU:0, one launch (start us, length us, event | category | flops | bytes accessed | tf_op | source)
XLA Modules:
  0.0 131.4 jit_solution(15096075007774949276)
XLA Ops:
  0.6 1.3 copy.64
  1.9 4.2 %all-to-all-start.6 = ((s32[4,4,8]{2,1,0:T(4,128)}), s32[4,4,8]{2,1,0:T(4,128)S(1)}, u32[]{:S(2)}, u32[]{:S(2)}) async-start(s32[4,4,8]{2,1,0:T(4,128)} %copy.64), calls=%async_computation.6 | async-start | bytes 16384 | tf_op jit(solution)/shard_map/all_to_all | solution.py:94
  6.2 0.7 fusion.13
  6.9 32.6 %all_gather.3 = bf16[64,16,256]{2,1,0:T(8,128)(2,1)S(1)} all-gather(bf16[8,16,256]{2,1,0:T(8,128)(2,1)} %param.7), channel_id=1, replica_groups=mesh['blk'=8,'frames'=4] {'blk'}, dimensions={0}, use_global_device_ids=true | all-gather | bytes 589824 | tf_op jit(solution)/shard_map/all_gather | solution.py:59
  39.5 4.0 %bitcast_reduce_fusion = (f32[4,1024]{1,0:T(4,128)S(1)}, f32[4,1020,1024]{2,1,0:T(8,128)S(1)}) fusion(bf16[1024,256,1]{1,0,2:T(8,128)(2,1)S(1)} %bitcast.96, bf16[4,1020,256]{2,0,1:T(4,128)(2,1)} %param.8), kind=kOutput, calls=%fused_computation.3 | convolution fusion | flops 2147446784 | bytes 19341312 | tf_op jit(solution)/shard_map/rc,fpc->frp/dot_general | solution.py:65
  43.5 5.9 %multiply_reduce_fusion.1 = (f32[4,1024]{1,0:T(4,128)S(1)}, f32[4,1024]{1,0:T(4,128)S(1)}, f32[4,1024]{1,0:T(4,128)S(1)}) fusion(f32[4,1020,1024]{2,1,0:T(8,128)S(1)} %get-tuple-element.24, f32[1020]{0:T(1024)S(1)} %get-tuple-element.25, f32[4,1024]{1,0:T(4,128)S(1)} %get-tuple-element.23, f32[1020]{0:T(1024)S(1)} %get-tuple-element.26), kind=kLoop, calls=%fused_computation.6 | loop fusion | flops 29233152 | bytes 16785376 | tf_op jit(solution)/shard_map/reduce_sum | solution.py:71
  50.0 3.2 %all-to-all-start.4 = ((s32[4,4,8]{2,1,0:T(4,128)}), s32[4,4,8]{2,1,0:T(4,128)S(1)}, u32[]{:S(2)}, u32[]{:S(2)}) async-start(s32[4,4,8]{2,1,0:T(4,128)} %copy.60), calls=%async_computation.4 | async-start | bytes 16384 | tf_op jit(solution)/shard_map/all_to_all | solution.py:95
  53.4 0.7 reshape.229
  54.2 2.8 %all-to-all-done.4 = s32[4,4,8]{2,1,0:T(4,128)S(1)} async-done(((s32[4,4,8]{2,1,0:T(4,128)}), s32[4,4,8]{2,1,0:T(4,128)S(1)}, u32[]{:S(2)}, u32[]{:S(2)}) %all-to-all-start.4) | async-done | bytes 544 | tf_op jit(solution)/shard_map/all_to_all | solution.py:95
  57.0 5.4 %all-to-all-start = ((f32[8,1,512]{2,1,0:T(1,128)}), f32[8,1,512]{2,1,0:T(1,128)S(1)}, u32[]{:S(2)}, u32[]{:S(2)}) async-start(f32[8,1,512]{2,1,0:T(1,128)} %reshape.229), calls=%async_computation | async-start | bytes 32768 | tf_op jit(solution)/shard_map/all_to_all | solution.py:79
  62.6 0.7 reshape.231
  63.4 5.6 %all-to-all-done = f32[8,1,512]{2,1,0:T(1,128)S(1)} async-done(((f32[8,1,512]{2,1,0:T(1,128)}), f32[8,1,512]{2,1,0:T(1,128)S(1)}, u32[]{:S(2)}, u32[]{:S(2)}) %all-to-all-start) | async-done | bytes 16416 | tf_op jit(solution)/shard_map/all_to_all | solution.py:79
  69.0 3.3 %all-to-all-start.1 = ((f32[8,1,512]{2,1,0:T(1,128)}), f32[8,1,512]{2,1,0:T(1,128)S(1)}, u32[]{:S(2)}, u32[]{:S(2)}) async-start(f32[8,1,512]{2,1,0:T(1,128)} %reshape.231), calls=%async_computation.1 | async-start | bytes 32768 | tf_op jit(solution)/shard_map/all_to_all | solution.py:77
  72.5 0.7 reshape.233
  73.3 5.6 %all-to-all-done.1 = f32[8,1,512]{2,1,0:T(1,128)S(1)} async-done(((f32[8,1,512]{2,1,0:T(1,128)}), f32[8,1,512]{2,1,0:T(1,128)S(1)}, u32[]{:S(2)}, u32[]{:S(2)}) %all-to-all-start.1) | async-done | bytes 16416 | tf_op jit(solution)/shard_map/all_to_all | solution.py:77
  78.8 3.3 %all-to-all-start.2 = ((f32[8,1,512]{2,1,0:T(1,128)}), f32[8,1,512]{2,1,0:T(1,128)S(1)}, u32[]{:S(2)}, u32[]{:S(2)}) async-start(f32[8,1,512]{2,1,0:T(1,128)} %reshape.233), calls=%async_computation.2 | async-start | bytes 32768 | tf_op jit(solution)/shard_map/all_to_all | solution.py:78
  82.4 0.7 reshape.235
  83.5 4.5 %gather_fusion = bf16[128,64,128]{2,1,0:T(8,128)(2,1)} fusion(bf16[4,64,64,128]{3,2,1,0:T(8,128)(2,1)} %param.10, s32[128]{0:T(128)S(1)} %reshape.216), kind=kCustom, calls=%fused_computation | custom fusion | bytes 4195328 | tf_op jit(solution)/shard_map/gather | solution.py:90
  88.7 5.3 %all-to-all-start.3 = ((f32[8,1,512]{2,1,0:T(1,128)}), f32[8,1,512]{2,1,0:T(1,128)S(1)}, u32[]{:S(2)}, u32[]{:S(2)}) async-start(f32[8,1,512]{2,1,0:T(1,128)} %reshape.235), calls=%async_computation.3 | async-start | bytes 32768 | tf_op jit(solution)/shard_map/all_to_all | solution.py:80
  94.0 6.6 %all-to-all-done.3 = f32[8,1,512]{2,1,0:T(1,128)S(1)} async-done(((f32[8,1,512]{2,1,0:T(1,128)}), f32[8,1,512]{2,1,0:T(1,128)S(1)}, u32[]{:S(2)}, u32[]{:S(2)}) %all-to-all-start.3) | async-done | bytes 16416 | tf_op jit(solution)/shard_map/all_to_all | solution.py:80
  100.5 3.6 %all-to-all-start.5 = ((bf16[4,4,8,64,128]{4,3,2,1,0:T(8,128)(2,1)}), bf16[4,4,8,64,128]{4,3,2,1,0:T(8,128)(2,1)S(1)}, u32[]{:S(2)}, u32[]{:S(2)}) async-start(bf16[4,4,8,64,128]{4,3,2,1,0:T(8,128)(2,1)} %bitcast.25), calls=%async_computation.5 | async-start | bytes 4194304 | tf_op jit(solution)/shard_map/all_to_all | solution.py:93
  106.1 0.7 reduce.2
  109.7 20.1 %all-to-all-done.5 = bf16[4,4,8,64,128]{4,3,2,1,0:T(8,128)(2,1)S(1)} async-done(((bf16[4,4,8,64,128]{4,3,2,1,0:T(8,128)(2,1)}), bf16[4,4,8,64,128]{4,3,2,1,0:T(8,128)(2,1)S(1)}, u32[]{:S(2)}, u32[]{:S(2)}) %all-to-all-start.5) | async-done | bytes 2097184 | tf_op jit(solution)/shard_map/all_to_all | solution.py:93
  129.8 0.8 multiply_reduce_fusion.6
  (63 shorter events, 8.0 us)
Async XLA Ops:
  0.6 129.2 %copy-start = (bf16[2,128]{1,0:T(2,128)(2,1)S(1)}, bf16[2,128]{1,0:T(2,128)(2,1)}, u32[]{:S(2)}) copy-start(bf16[2,128]{1,0:T(2,128)(2,1)} %param.9) | copy-start | bytes 1540
  1.9 48.1 %all-to-all-start.6 = ((s32[4,4,8]{2,1,0:T(4,128)}), s32[4,4,8]{2,1,0:T(4,128)S(1)}, u32[]{:S(2)}, u32[]{:S(2)}) async-start(s32[4,4,8]{2,1,0:T(4,128)} %copy.64), calls=%async_computation.6 | async-start | bytes 16384 | tf_op jit(solution)/shard_map/all_to_all | solution.py:94
  43.5 5.9 %copy-start.1 = (s32[4,1,4,8]{3,2,1,0:T(4,128)S(1)}, s32[4,1,4,8]{3,2,1,0:T(4,128)}, u32[]{:S(2)}) copy-start(s32[4,1,4,8]{3,2,1,0:T(4,128)} %param.13) | copy-start | bytes 1540
  43.5 10.7 %copy-start.2 = (s32[2,16,2]{1,2,0:T(2,128)S(1)}, s32[2,16,2]{1,2,0:T(2,128)}, u32[]{:S(2)}) copy-start(s32[2,16,2]{1,2,0:T(2,128)} %param.11) | copy-start | bytes 772
  50.0 7.0 %all-to-all-start.4 = ((s32[4,4,8]{2,1,0:T(4,128)}), s32[4,4,8]{2,1,0:T(4,128)S(1)}, u32[]{:S(2)}, u32[]{:S(2)}) async-start(s32[4,4,8]{2,1,0:T(4,128)} %copy.60), calls=%async_computation.4 | async-start | bytes 16384 | tf_op jit(solution)/shard_map/all_to_all | solution.py:95
  57.0 11.9 %all-to-all-start = ((f32[8,1,512]{2,1,0:T(1,128)}), f32[8,1,512]{2,1,0:T(1,128)S(1)}, u32[]{:S(2)}, u32[]{:S(2)}) async-start(f32[8,1,512]{2,1,0:T(1,128)} %reshape.229), calls=%async_computation | async-start | bytes 32768 | tf_op jit(solution)/shard_map/all_to_all | solution.py:79
  69.0 9.8 %all-to-all-start.1 = ((f32[8,1,512]{2,1,0:T(1,128)}), f32[8,1,512]{2,1,0:T(1,128)S(1)}, u32[]{:S(2)}, u32[]{:S(2)}) async-start(f32[8,1,512]{2,1,0:T(1,128)} %reshape.231), calls=%async_computation.1 | async-start | bytes 32768 | tf_op jit(solution)/shard_map/all_to_all | solution.py:77
  78.8 9.9 %all-to-all-start.2 = ((f32[8,1,512]{2,1,0:T(1,128)}), f32[8,1,512]{2,1,0:T(1,128)S(1)}, u32[]{:S(2)}, u32[]{:S(2)}) async-start(f32[8,1,512]{2,1,0:T(1,128)} %reshape.233), calls=%async_computation.2 | async-start | bytes 32768 | tf_op jit(solution)/shard_map/all_to_all | solution.py:78
  88.7 11.9 %all-to-all-start.3 = ((f32[8,1,512]{2,1,0:T(1,128)}), f32[8,1,512]{2,1,0:T(1,128)S(1)}, u32[]{:S(2)}, u32[]{:S(2)}) async-start(f32[8,1,512]{2,1,0:T(1,128)} %reshape.235), calls=%async_computation.3 | async-start | bytes 32768 | tf_op jit(solution)/shard_map/all_to_all | solution.py:80
  100.5 29.2 %all-to-all-start.5 = ((bf16[4,4,8,64,128]{4,3,2,1,0:T(8,128)(2,1)}), bf16[4,4,8,64,128]{4,3,2,1,0:T(8,128)(2,1)S(1)}, u32[]{:S(2)}, u32[]{:S(2)}) async-start(bf16[4,4,8,64,128]{4,3,2,1,0:T(8,128)(2,1)} %bitcast.25), calls=%async_computation.5 | async-start | bytes 4194304 | tf_op jit(solution)/shard_map/all_to_all | solution.py:93
where the time goes:
time: 132 us; the launch traced here: 131 us
  waiting for transfers between devices  41.3 us (31%)
  blocking collectives  32.6 us (25%)
  starting transfers between devices  28.4 us (22%)
  local copies, waits for them, and re-layouts  12.4 us (9%)
  other arithmetic  10.9 us (8%)
  matrix products  4.82 us (4%)
    all_gather x1, blocking collectives, body(): shard_piece = lax.all_gather(coarse_query, 'blk', axis=0, tiled=True)  32.6 us
    all_to_all x1, waiting for transfers between devices, body(): lax.all_to_all(picked, 'frames', split_axis=0, concat_axis=0, tiled=True)  20.1 us
    all_to_all x1, waiting for transfers between devices, body(): lax.all_to_all(stats[3][None], 'blk', split_axis=2, concat_axis=0, tiled=...  6.56 us
    reduce_sum x1, other arithmetic, body(): row_sums = jnp.sum(weights * local_row[None, None, :], axis=2)  5.89 us
    all_to_all x1, waiting for transfers between devices, body(): lax.all_to_all(stats[2][None], 'blk', split_axis=2, concat_axis=0, tiled=...  5.63 us
    all_to_all x1, waiting for transfers between devices, body(): lax.all_to_all(stats[0][None], 'blk', split_axis=2, concat_axis=0, tiled=...  5.56 us
    all_to_all x1, starting transfers between devices, body(): lax.all_to_all(stats[2][None], 'blk', split_axis=2, concat_axis=0, tiled=...  5.37 us
    all_to_all x1, starting transfers between devices, body(): lax.all_to_all(stats[3][None], 'blk', split_axis=2, concat_axis=0, tiled=...  5.29 us
  transfers between devices with their start and end apart: 7, of which 6 were waited for; matrix products, arithmetic and copies ran while one was open for 19% of the time, Pallas kernels for 0%

commit v1 on v0

v1 whole, which is shorter than its diff:
```python
import functools
import math

import jax
import jax.numpy as jnp
from jax import lax
from jax.experimental import pallas as pl
from jax.experimental.pallas import tpu as pltpu
from jax.sharding import PartitionSpec as P

GH = 68
GW = 120
TILE = 8
LOW = -3e38
spread_cells = 32.0

VMEM = pl.BlockSpec(memory_space=pltpu.VMEM)
SMEM = pl.BlockSpec(memory_space=pltpu.SMEM)


def pack_kernel(query_ref, pos_ref, out_ref):
    tracks = query_ref.shape[0]
    window = pos_ref.shape[1]
    lanes = out_ref.shape[1]
    out_ref[...] = jnp.zeros(out_ref.shape, jnp.float32)
    out_ref[0:tracks, :] = query_ref[...].astype(jnp.float32)
    eye = (
        lax.broadcasted_iota(jnp.int32, (window, lanes), 0)
        == lax.broadcasted_iota(jnp.int32, (window, lanes), 1)
    ).astype(jnp.float32)
    for k in range(2):
        out_ref[(k + 1) * tracks : (k + 2) * tracks, :] = lax.dot_general(
            pos_ref[k].astype(jnp.float32),
            eye,
            (((0,), (0,)), ((), ())),
            precision=lax.Precision.HIGHEST,
            preferred_element_type=jnp.float32,
        )


def pack_tracks(fine_query, track_pos):
    return pl.pallas_call(
        pack_kernel,
        out_shape=jax.ShapeDtypeStruct((8, fine_query.shape[1]), jnp.float32),
        in_specs=[VMEM, VMEM],
        out_specs=VMEM,
        name="pack_tracks",
    )(fine_query, track_pos)


def fine_kernel(pieces, own, place_ref, ids_ref, list_ref, valid_ref, tiles_ref, *refs):
    ins, outs = refs[:pieces], refs[pieces:]
    frames, _, cells, channels = tiles_ref.shape
    slots = list_ref.shape[3]
    tracks = pieces * own
    wide = slots * cells
    base = place_ref[0]
    me = place_ref[1]
    scale = 1.0 / math.sqrt(channels)
    query = jnp.concatenate([r[0:own, :] for r in ins], axis=0).astype(jnp.bfloat16)
    rows_in = jnp.concatenate([r[own : 2 * own, :] for r in ins], axis=0)
    cols_in = jnp.concatenate([r[2 * own : 3 * own, :] for r in ins], axis=0)
    lane_in = lax.broadcasted_iota(jnp.int32, (tracks, channels), 1)
    spread = (
        lax.broadcasted_iota(jnp.int32, (slots, wide), 0)
        == lax.broadcasted_iota(jnp.int32, (slots, wide), 1) // cells
    ).astype(jnp.bfloat16)
    inner = lax.broadcasted_iota(jnp.int32, (tracks, wide), 1) % cells
    inner_row = (inner // TILE).astype(jnp.float32)
    inner_col = (inner % TILE).astype(jnp.float32)
    piece_wide = lax.broadcasted_iota(jnp.int32, (tracks, wide), 0) // own
    piece_slot = lax.broadcasted_iota(jnp.int32, (tracks, slots), 0) // own
    lane_out = lax.broadcasted_iota(jnp.int32, (tracks, 2 * frames), 1)
    result = jnp.zeros((tracks, 2 * frames), jnp.float32)
    for i in range(frames):
        scores = jnp.zeros((tracks, wide), jnp.float32)
        codes = jnp.zeros((tracks, slots), jnp.float32)
        for j in range(pieces):
            owner = lax.bitwise_xor(me, j)
            block = jnp.concatenate(
                [tiles_ref[i, ids_ref[i, 0, owner, s]] for s in range(slots)], axis=0
            )
            got = lax.dot_general(
                query, block, (((1,), (1,)), ((), ())), preferred_element_type=jnp.float32
            )
            scores = jnp.where(piece_wide == j, got, scores)
            ids = list_ref[i, 0, pl.ds(owner, 1), :]
            live = valid_ref[i, 0, pl.ds(owner, 1), :]
            code = jnp.where(live > 0, ids, -1).astype(jnp.float32)
            codes = jnp.where(piece_slot == j, jnp.broadcast_to(code, (tracks, slots)), codes)
        code = lax.dot_general(
            codes.astype(jnp.bfloat16),
            spread,
            (((1,), (0,)), ((), ())),
            preferred_element_type=jnp.float32,
        )
        cell = code + base.astype(jnp.float32)
        tile_row = jnp.floor((cell + 0.5) * (1.0 / GW))
        tile_col = cell - GW * tile_row
        here = lane_in == me * frames + i
        track_row = jnp.sum(jnp.where(here, rows_in, 0.0), axis=1, keepdims=True)
        track_col = jnp.sum(jnp.where(here, cols_in, 0.0), axis=1, keepdims=True)
        off_row = (tile_row * TILE + inner_row) - track_row
        off_col = (tile_col * TILE + inner_col) - track_col
        distance = off_row * off_row + off_col * off_col
        scores = scores * scale - distance * (0.5 / (spread_cells * spread_cells))
        scores = jnp.where(code < -0.5, -1e30, scores)
        highest = jnp.max(scores, axis=1, keepdims=True)
        weights = jnp.exp(scores - highest)
        norm = 1.0 / (jnp.sum(weights, axis=1, keepdims=True) * spread_cells)
        mean_row = jnp.sum(weights * off_row, axis=1, keepdims=True) * norm
        mean_col = jnp.sum(weights * off_col, axis=1, keepdims=True) * norm
        result = jnp.where(lane_out == i, mean_row, result)
        result = jnp.where(lane_out == frames + i, mean_col, result)
    eye = (
        lax.broadcasted_iota(jnp.int32, (tracks, tracks), 0)
        == lax.broadcasted_iota(jnp.int32, (tracks, tracks), 1)
    ).astype(jnp.float32)
    turned = lax.dot_general(
        result,
        eye,
        (((0,), (0,)), ((), ())),
        precision=lax.Precision.HIGHEST,
        preferred_element_type=jnp.float32,
    )
    for j in range(pieces):
        for k in range(2):
            outs[j][k] = turned[k * frames : (k + 1) * frames, j * own : (j + 1) * own]


def fine_part(place, tile_list, tile_valid, fine_tiles, own, payloads):
    pieces = len(payloads)
    frames = fine_tiles.shape[0]
    return pl.pallas_call(
        functools.partial(fine_kernel, pieces, own),
        out_shape=[jax.ShapeDtypeStruct((2, frames, own), jnp.float32)] * pieces,
        in_specs=[SMEM, SMEM, VMEM, VMEM, VMEM] + [VMEM] * pieces,
        out_specs=[VMEM] * pieces,
        name="fine_part",
    )(place, tile_list, tile_list, tile_valid, fine_tiles, *payloads)


def coarse_kernel(half, region, place_ref, q_ref, f_ref, *rest):
    if half:
        prev_ref, o_ref, s0, s1 = rest
    else:
        o_ref, s0, s1 = rest
    frames = f_ref.shape[0]
    groups, rows, channels = q_ref.shape
    per = 256 // rows
    quads = groups // per
    steps = frames * quads
    padded = s0.shape[0]
    tiles = padded // 8
    line = GW // 8
    factor = math.log2(math.e) / math.sqrt(channels)
    base = place_ref[0]
    row0 = base // GW
    col0 = base - row0 * GW
    tail = padded - region
    if tail:
        for s in (s0, s1):
            s[padded - 8 : padded, :] = jnp.full((8, 256), LOW, jnp.float32)

    def scores(step, s):
        frame = step // quads
        quad = step % quads
        q = q_ref[pl.ds(quad * per, per)].reshape(256, channels)
        best = jnp.full((8, 256), LOW, jnp.float32)
        for at in range(0, region, 240):
            n = min(240, region - at)
            d = lax.dot_general(
                f_ref[frame, at : at + n, :],
                q,
                (((1,), (1,)), ((), ())),
                preferred_element_type=jnp.float32,
            )
            s[at : at + n, :] = d
            full = n // 8 * 8
            best = jnp.maximum(best, jnp.max(d[:full].reshape(full // 8, 8, 256), axis=0))
        if tail:
            best = jnp.maximum(best, s[padded - 8 : padded, :])
        return jnp.max(best, axis=0, keepdims=True)

    sub = lax.broadcasted_iota(jnp.int32, (8, 128), 0)

    def sums(step, s, best):
        frame = step // quads
        quad = step % quads
        for lt in range(2):
            m = jnp.broadcast_to(best[:, lt * 128 : (lt + 1) * 128], (8, 128))
            cols = [None] * line
            row_sum = jnp.zeros((8, 128), jnp.float32)
            for r in range(pl.cdiv(tiles, line)):
                acc = None
                for j in range(min(line, tiles - r * line)):
                    i = r * line + j
                    p = jnp.exp2((s[8 * i : 8 * i + 8, lt * 128 : (lt + 1) * 128] - m) * factor)
                    cols[j] = p if cols[j] is None else cols[j] + p
                    acc = p if acc is None else acc + p
                if r:
                    row_sum = row_sum + acc * float(r)
            total = None
            col_sum = jnp.zeros((8, 128), jnp.float32)
            for j in range(min(line, tiles)):
                total = cols[j] if total is None else total + cols[j]
                local = sub + (8 * j + col0)
                over = (local >= GW).astype(jnp.float32)
                at = local.astype(jnp.float32) - (GW - 1) / 2.0 - GW * over
                col_sum = col_sum + cols[j] * at
                row_sum = row_sum + cols[j] * over
            row_sum = row_sum + total * (row0.astype(jnp.float32) - (GH - 1) / 2.0)
            stats = [m[0:1]] + [
                jnp.sum(v, axis=0, keepdims=True) for v in (total, row_sum, col_sum)
            ]
            width = min(rows, 128)
            for k in range(128 // width):
                column = lt * 128 + k * width
                group = quad * per + column // rows
                lane = half * rows + column % rows
                for st in range(4):
                    o_ref[
                        group, lane // 128, pl.ds(st * frames + frame, 1), lane % 128 : lane % 128 + width
                    ] = stats[st][:, k * width : (k + 1) * width]

    if half:
        if rows < 128:
            o_ref[:, :, :, 0:rows] = prev_ref[:, :, :, 0:rows]
        else:
            o_ref[:, 0 : rows // 128] = prev_ref[:, 0 : rows // 128]

    def turn(i, best0):
        best1 = scores(2 * i + 1, s1)
        sums(2 * i, s0, best0)
        following = scores(jnp.minimum(2 * i + 2, steps - 1), s0)
        sums(2 * i + 1, s1, best1)
        return following

    lax.fori_loop(0, steps // 2, turn, scores(0, s0))


def coarse_half(place, q, f, prev=None):
    frames, region, channels = f.shape
    groups, rows, _ = q.shape
    half = 0 if prev is None else 1
    padded = pl.cdiv(region, 8) * 8
    return pl.pallas_call(
        functools.partial(coarse_kernel, half, region),
        out_shape=jax.ShapeDtypeStruct((groups, rows // 64, 4 * frames, 128), jnp.float32),
        in_specs=[SMEM, VMEM, VMEM] + [VMEM] * half,
        out_specs=VMEM,
        scratch_shapes=[pltpu.VMEM((padded, 256), jnp.float32)] * 2,
        name=f"coarse_half_{half}",
    )(place, q, f, *([prev] if half else []))


def finish_kernel(pieces, heads, channels, place_ref, stats_ref, *refs):
    scale = math.log2(math.e) / math.sqrt(channels)
    ins, (coarse_ref, fine_ref) = refs[:pieces], refs[pieces:]
    me = place_ref[1]
    sources, tiles, quarter, _ = stats_ref.shape
    frames = quarter // 4
    rows = tiles * 128
    tracks = rows // heads

    def take(d, st):
        return jnp.concatenate(
            [stats_ref[d, t, st * frames : (st + 1) * frames, :] for t in range(tiles)], axis=1
        )

    top = take(0, 0)
    for d in range(1, sources):
        top = jnp.maximum(top, take(d, 0))
    total = jnp.zeros((frames, rows), jnp.float32)
    row = jnp.zeros((frames, rows), jnp.float32)
    col = jnp.zeros((frames, rows), jnp.float32)
    for d in range(sources):
        keep = jnp.exp2((take(d, 0) - top) * scale)
        total = total + take(d, 1) * keep
        row = row + take(d, 2) * keep
        col = col + take(d, 3) * keep
    core = lax.rem(me, 2)
    lane = lax.broadcasted_iota(jnp.int32, (rows, tracks), 0) // heads
    where = lax.broadcasted_iota(jnp.int32, (rows, tracks), 1)
    lane = jnp.where(lane < tracks // 2, lane + core * (tracks // 2), lane - core * (tracks // 2))
    mean = (lane == where).astype(jnp.float32)
    for k, (v, size) in enumerate(((row, GH), (col, GW))):
        coarse_ref[k] = lax.dot_general(
            v / total,
            mean,
            (((1,), (0,)), ((), ())),
            precision=lax.Precision.HIGHEST,
            preferred_element_type=jnp.float32,
        ) * (4.0 / (heads * size))
    for j in range(pieces):
        start = lax.bitwise_xor(me, j) * frames
        for k in range(2):
            fine_ref[k, pl.ds(start, frames), :] = ins[j][k]


def finish(place, stats, pieces, heads, channels, window):
    quarter = stats.shape[2]
    rows = stats.shape[1] * 128
    return pl.pallas_call(
        functools.partial(finish_kernel, len(pieces), heads, channels),
        out_shape=[
            jax.ShapeDtypeStruct((2, quarter // 4, rows // heads), jnp.float32),
            jax.ShapeDtypeStruct((2, window, pieces[0].shape[2]), jnp.float32),
        ],
        in_specs=[SMEM, VMEM] + [VMEM] * len(pieces),
        out_specs=[VMEM, VMEM],
        name="finish",
    )(place, stats, *pieces)


def body(coarse_query, coarse_feat, fine_query, fine_tiles, track_pos, tile_list, tile_valid):
    tracks, heads, channels = coarse_query.shape
    blocks = lax.axis_size("blk")
    owners = lax.axis_size("frames")
    region = coarse_feat.shape[1]
    window = track_pos.shape[1]
    own = fine_query.shape[0]
    me = lax.axis_index("frames").astype(jnp.int32)
    base = lax.axis_index("blk").astype(jnp.int32) * region
    place = jnp.stack([base, me])

    def swap(x, j):
        return lax.ppermute(x, "frames", [(i, i ^ j) for i in range(owners)])

    halves = coarse_query.reshape(2, tracks * heads // 2, channels)
    mine = lax.dynamic_index_in_dim(halves, lax.rem(me, 2), 0, keepdims=True)
    mine = jnp.broadcast_to(mine, (blocks,) + mine.shape[1:])
    first = lax.all_to_all(mine, "blk", split_axis=0, concat_axis=0, tiled=True)

    payload = pack_tracks(fine_query, track_pos)
    payloads = [payload] + [swap(payload, j) for j in range(1, owners)]
    fine = fine_part(place, tile_list, tile_valid, fine_tiles, own, payloads)
    fine = [fine[0]] + [swap(fine[j], j) for j in range(1, owners)]

    second = swap(first, 1)
    stats = coarse_half(place, first, coarse_feat)
    stats = coarse_half(place, second, coarse_feat, stats)
    stats = lax.all_to_all(stats, "blk", split_axis=0, concat_axis=0, tiled=True)
    return tuple(finish(place, stats, fine, heads, channels, window))


def solution(mesh):
    return jax.shard_map(
        body,
        mesh=mesh,
        in_specs=(
            P("blk", None, None),
            P("frames", "blk", None),
            P(("blk", "frames"), None),
            P("frames", "blk", None, None),
            P(None, None, ("blk", "frames")),
            P("frames", "blk", None, None),
            P("frames", "blk", None, None),
        ),
        out_specs=(P(None, "frames", "blk"), P(None, None, ("blk", "frames"))),
        check_vma=False,
    )
```

time: 132 us -> 58.4 us (0.44)
  waiting for transfers between devices: 41.3 us -> 5.67 us
  starting transfers between devices: 28.4 us -> 7.33 us
  Pallas kernels: 0 us -> 19.4 us
  blocking collectives: 32.6 us -> 16 us
  other arithmetic: 10.9 us -> 0.55 us
  matrix products: 4.82 us -> 0 us
  local copies, waits for them, and re-layouts: 12.4 us -> 8.14 us
    all_to_all x7 -> x1, waiting for transfers between devices: 41.3 us -> 0.01 us  [body(): lax.all_to_all(stats, 'blk', split_axis=0, concat_axis=0, tiled=True)]
    all_gather x1 -> x0, blocking collectives: 32.6 us -> none  [body(): shard_piece = lax.all_gather(coarse_query, 'blk', axis=0, tiled=True)]
    all_to_all x7 -> x1, starting transfers between devices: 28.4 us -> 3.6 us  [body(): lax.all_to_all(stats, 'blk', split_axis=0, concat_axis=0, tiled=True)]
    pallas_call x0 -> x5, Pallas kernels: none -> 19.4 us  [the longest x2 12.2 us: coarse_half(): pl.pallas_call(functools.partial(coarse_kernel, half, region), out_shape=...]
    all_to_all x0 -> x1, blocking collectives: none -> 16 us  [body(): first = lax.all_to_all(mine, 'blk', split_axis=0, concat_axis=0, tiled=True)]
    reduce_sum x3 -> x0, other arithmetic: 6.13 us -> none  [the longest x1 5.89 us: body(): row_sums = jnp.sum(weights * local_row[None, None, :], axis=2)]
    ppermute x0 -> x7, waiting for transfers between devices: none -> 5.67 us  [swap(): return lax.ppermute(x, 'frames', [(i, i ^ j) for i in range(owners)])]
    gather x1 -> x0, local copies, waits for them, and re-layouts: 4.49 us -> none  [body(): fine_tiles[jnp.arange(frames_here, dtype=jnp.int32)[None, :, None], list_...]
  transfers between devices with their start and end apart: 7 -> 8, of which waited for: 6 -> 4; matrix products, arithmetic and copies ran while one was open for 19% -> 8% of each run, Pallas kernels for 0% -> 20%
where the time goes in v1:
time: 58.4 us; the launch traced here: 57.8 us
  Pallas kernels  19.4 us (33%)
  blocking collectives  16 us (27%)
  local copies, waits for them, and re-layouts  8.14 us (14%)
  starting transfers between devices  7.33 us (13%)
  waiting for transfers between devices  5.67 us (10%)
  between operations  0.68 us (1%)
    all_to_all x1, blocking collectives, body(): first = lax.all_to_all(mine, 'blk', split_axis=0, concat_axis=0, tiled=True)  16 us
    pallas_call x2, Pallas kernels, coarse_half(): pl.pallas_call(functools.partial(coarse_kernel, half, region), out_shape=...  12.2 us
    unnamed x24, local copies, waits for them, and re-layouts  6.74 us
    ppermute x7, waiting for transfers between devices, swap(): return lax.ppermute(x, 'frames', [(i, i ^ j) for i in range(owners)])  5.67 us
    pallas_call x1, Pallas kernels, fine_part(): pl.pallas_call(functools.partial(fine_kernel, pieces, own), out_shape=[ja...  4.01 us
    ppermute x7, starting transfers between devices, swap(): return lax.ppermute(x, 'frames', [(i, i ^ j) for i in range(owners)])  3.72 us
    all_to_all x1, starting transfers between devices, body(): lax.all_to_all(stats, 'blk', split_axis=0, concat_axis=0, tiled=True)  3.6 us
    pallas_call x1, Pallas kernels, finish(): pl.pallas_call(functools.partial(finish_kernel, len(pieces), heads, chann...  1.7 us
  transfers between devices with their start and end apart: 8, of which 4 were waited for; matrix products, arithmetic and copies ran while one was open for 8% of the time, Pallas kernels for 20%

profile of v1, /device:TPU:0, one launch (start us, length us, event | category | flops | bytes accessed | tf_op | source)
XLA Modules:
  0.0 57.8 jit_solution(9753581481509530817)
XLA Ops:
  0.7 0.8 %copy-done = bf16[8,16,256]{2,1,0:T(8,128)(2,1)S(1)} copy-done((bf16[8,16,256]{2,1,0:T(8,128)(2,1)S(1)}, bf16[8,16,256]{2,1,0:T(8,128)(2,1)}, u32[]{:S(2)}) %copy-start) | copy-done | bytes 65560
  1.5 16.0 %all_to_all.10.q_ref = bf16[8,64,256]{2,1,0:T(8,128)(2,1)S(1)} all-to-all(bf16[8,64,256]{2,1,0:T(8,128)(2,1)S(1)} %broadcast_in_dim.8), channel_id=1, replica_groups=mesh['blk'=8,'frames'=4] {'blk'}, dimensions={0} | all-to-all | bytes 524288 | tf_op jit(solution)/shard_map/all_to_all | solution.py:333
  17.5 3.3 %copy.10.f_ref = bf16[4,1020,256]{2,1,0:T(8,128)(2,1)} copy(bf16[4,1020,256]{2,0,1:T(4,128)(2,1)} %param.8) | data formatting | bytes 4177920 | tf_op args[1]
  20.8 0.6 pad_add_fusion.place_ref
  21.4 6.1 %coarse_half_0.1.rest_0_ = f32[8,1,16,128]{3,2,1,0:T(8,128)} custom-call(s32[2]{0:T(128)} %pad_add_fusion.place_ref, bf16[8,64,256]{2,1,0:T(8,128)(2,1)} %copy-done.1, bf16[4,1020,256]{2,1,0:T(8,128)(2,1)} %copy.10.f_ref), custom_call_target="tpu_custom_call" | custom-call | tf_op jit(solution)/shard_map/coarse_half_0/pallas_call | solution.py:247
  27.5 0.7 %copy-done.3 = bf16[8,64,256]{2,1,0:T(8,128)(2,1)} copy-done((bf16[8,64,256]{2,1,0:T(8,128)(2,1)}, bf16[8,64,256]{2,1,0:T(8,128)(2,1)S(1)}, u32[]{:S(2)}) %copy-start.3) | copy-done | bytes 262168
  28.2 6.0 %coarse_half_1.1 = f32[8,1,16,128]{3,2,1,0:T(8,128)} custom-call(s32[2]{0:T(128)} %pad_add_fusion.place_ref, bf16[8,64,256]{2,1,0:T(8,128)(2,1)} %copy-done.3, bf16[4,1020,256]{2,1,0:T(8,128)(2,1)} %copy.10.f_ref, f32[8,1,16,128]{3,2,1,0:T(8,128)} %coarse_half_0.1.rest_0_), custom_call_target="tpu_custom_call" | custom-call | tf_op jit(solution)/shard_map/coarse_half_1/pallas_call | solution.py:247
  34.3 3.6 %all-to-all-start.1 = ((f32[8,1,16,128]{3,2,1,0:T(8,128)}), f32[8,1,16,128]{3,2,1,0:T(8,128)S(1)}, u32[]{:S(2)}, u32[]{:S(2)}) async-start(f32[8,1,16,128]{3,2,1,0:T(8,128)} %coarse_half_1.1), calls=%async_computation.1 | async-start | bytes 131072 | tf_op jit(solution)/shard_map/all_to_all | solution.py:343
  37.9 0.7 %copy.11.pos_ref = s32[2,16,2]{2,1,0:T(8,128)} copy(s32[2,16,2]{1,2,0:T(2,128)S(1)} %copy-done.10) | data formatting | bytes 512 | tf_op args[4]
  38.6 1.5 %pack_tracks.1.refs_0_ = f32[8,128]{1,0:T(8,128)} custom-call(bf16[2,128]{1,0:T(2,128)(2,1)} %query_ref.1, s32[2,16,2]{2,1,0:T(8,128)} %copy.11.pos_ref), custom_call_target="tpu_custom_call" | custom-call | tf_op jit(solution)/shard_map/pack_tracks/pallas_call | solution.py:42
  40.1 0.2 collective-permute-start.1
  40.3 1.5 %collective-permute-start.2 = (f32[8,128]{1,0:T(8,128)}, f32[8,128]{1,0:T(8,128)S(1)}, u32[]{:S(2)}, u32[]{:S(2)}) collective-permute-start(f32[8,128]{1,0:T(8,128)} %pack_tracks.1.refs_0_), channel_id=1, source_target_pairs={{0,2},{1,3},{2,0},{3,1},{4,6},{5,7},{6,4},{7,5},{8,10},{9,11},{10,... | collective-permute-start | bytes 12296 | tf_op jit(solution)/shard_map/ppermute | solution.py:328
  41.8 0.2 collective-permute-start.3
  42.0 2.1 %collective-permute-done.2.refs_2_ = f32[8,128]{1,0:T(8,128)S(1)} collective-permute-done((f32[8,128]{1,0:T(8,128)}, f32[8,128]{1,0:T(8,128)S(1)}, u32[]{:S(2)}, u32[]{:S(2)}) %collective-permute-start.2) | collective-permute-done | bytes 4128 | tf_op jit(solution)/shard_map/ppermute | solution.py:328
  44.1 0.9 %collective-permute-done.3.refs_3_ = f32[8,128]{1,0:T(8,128)S(1)} collective-permute-done((f32[8,128]{1,0:T(8,128)}, f32[8,128]{1,0:T(8,128)S(1)}, u32[]{:S(2)}, u32[]{:S(2)}) %collective-permute-start.3) | collective-permute-done | bytes 4128 | tf_op jit(solution)/shard_map/ppermute | solution.py:328
  45.0 0.6 %copy-done.9 = f32[8,128]{1,0:T(8,128)} copy-done((f32[8,128]{1,0:T(8,128)}, f32[8,128]{1,0:T(8,128)S(1)}, u32[]{:S(2)}) %copy-start.9) | copy-done | bytes 4120
  45.6 4.0 %fine_part.1 = (f32[2,4,2]{2,1,0:T(4,128)}, f32[2,4,2]{2,1,0:T(4,128)}, f32[2,4,2]{2,1,0:T(4,128)}, f32[2,4,2]{2,1,0:T(4,128)}) custom-call(s32[2]{0:T(128)} %pad_add_fusion.place_ref, s32[4,1,4,8]{3,2,1,0:T(4,128)} %list_ref.1, s32[4,1,4,8]{3,2,1,0:T(4,128)} %list_ref.1, s32[4,1,4,8]{3,2,1,0:T(4,128)} %valid_ref.1, bf16[4,64,64,128]{3,2,1,0:T(8,128)(2,1)} %tiles_ref.1, ...), custom_call_target="tpu_custom_call" | custom-call | tf_op jit(solution)/shard_map/fine_part/pallas_call | solution.py:134
  49.8 1.1 %collective-permute-start.5 = (f32[2,4,2]{2,1,0:T(4,128)}, f32[2,4,2]{2,1,0:T(4,128)S(1)}, u32[]{:S(2)}, u32[]{:S(2)}) collective-permute-start(f32[2,4,2]{2,1,0:T(4,128)} %get-tuple-element.8), channel_id=1, source_target_pairs={{0,2},{1,3},{2,0},{3,1},{4,6},{5,7},{6,4},{7,5},{8,10},{9,11},{10,... | collective-permute-start | bytes 200 | tf_op jit(solution)/shard_map/ppermute | solution.py:328
  50.9 0.6 %collective-permute-start.6 = (f32[2,4,2]{2,1,0:T(4,128)}, f32[2,4,2]{2,1,0:T(4,128)S(1)}, u32[]{:S(2)}, u32[]{:S(2)}) collective-permute-start(f32[2,4,2]{2,1,0:T(4,128)} %get-tuple-element.9), channel_id=1, source_target_pairs={{0,3},{1,2},{2,1},{3,0},{4,7},{5,6},{6,5},{7,4},{8,11},{9,10},{10,... | collective-permute-start | bytes 200 | tf_op jit(solution)/shard_map/ppermute | solution.py:328
  51.5 2.1 %collective-permute-done.5.refs_2_ = f32[2,4,2]{2,1,0:T(4,128)S(1)} collective-permute-done((f32[2,4,2]{2,1,0:T(4,128)}, f32[2,4,2]{2,1,0:T(4,128)S(1)}, u32[]{:S(2)}, u32[]{:S(2)}) %collective-permute-start.5) | collective-permute-done | bytes 96 | tf_op jit(solution)/shard_map/ppermute | solution.py:328
  53.6 0.5 collective-permute-done.6.refs_3_
  54.2 0.5 copy-done.6
  54.7 1.7 %finish.1 = (f32[2,4,8]{2,1,0:T(4,128)}, f32[2,16,2]{2,1,0:T(8,128)}) custom-call(s32[2]{0:T(128)} %pad_add_fusion.place_ref, f32[8,1,16,128]{3,2,1,0:T(8,128)} %copy-done.2, f32[2,4,2]{2,1,0:T(4,128)} %get-tuple-element.6.refs_0_, f32[2,4,2]{2,1,0:T(4,128)} %copy-done.4, f32[2,4,2]{2,1,0:T(4,128)} %copy-done.5, f32[2,4,2]{2,1,0:T(4,128)} %copy-done.6), custom_call_target="tpu_custom_call" | custom-call | tf_op jit(solution)/shard_map/finish/pallas_call | solution.py:304
  56.4 1.4 %copy.12 = f32[2,16,2]{1,2,0:T(2,128)} copy(f32[2,16,2]{2,1,0:T(8,128)} %get-tuple-element.11) | data formatting | bytes 512 | tf_op jit(solution)/shard_map/finish/pallas_call | solution.py:304
  (26 shorter events, 0.3 us)
Async XLA Ops:
  0.6 0.8 %copy-start = (bf16[8,16,256]{2,1,0:T(8,128)(2,1)S(1)}, bf16[8,16,256]{2,1,0:T(8,128)(2,1)}, u32[]{:S(2)}) copy-start(bf16[8,16,256]{2,1,0:T(8,128)(2,1)} %param.7) | copy-start | bytes 196612
  17.5 3.3 %copy-start.1 = (bf16[8,64,256]{2,1,0:T(8,128)(2,1)}, bf16[8,64,256]{2,1,0:T(8,128)(2,1)S(1)}, u32[]{:S(2)}) copy-start(bf16[8,64,256]{2,1,0:T(8,128)(2,1)S(1)} %all_to_all.10.q_ref) | copy-start | bytes 786436
  17.5 10.0 %collective-permute-start = (bf16[8,64,256]{2,1,0:T(8,128)(2,1)S(1)}, bf16[8,64,256]{2,1,0:T(8,128)(2,1)S(1)}, u32[]{:S(2)}, u32[]{:S(2)}) collective-permute-start(bf16[8,64,256]{2,1,0:T(8,128)(2,1)S(1)} %all_to_all.10.q_ref), channel_id=1, source_target_pairs={{0,1},{1,0},{2,3},{3,2},{4,5},{5,4},{6,7},{7,6},{8,9},{9,8},{10,11... | collective-permute-start | bytes 786440 | tf_op jit(solution)/shard_map/ppermute | solution.py:328
  21.4 16.5 %copy-start.10 = (s32[2,16,2]{1,2,0:T(2,128)S(1)}, s32[2,16,2]{1,2,0:T(2,128)}, u32[]{:S(2)}) copy-start(s32[2,16,2]{1,2,0:T(2,128)} %param.11) | copy-start | bytes 772
  27.5 0.7 %copy-start.3 = (bf16[8,64,256]{2,1,0:T(8,128)(2,1)}, bf16[8,64,256]{2,1,0:T(8,128)(2,1)S(1)}, u32[]{:S(2)}) copy-start(bf16[8,64,256]{2,1,0:T(8,128)(2,1)S(1)} %collective-permute-done.q_ref) | copy-start | bytes 786436
  34.3 19.9 %all-to-all-start.1 = ((f32[8,1,16,128]{3,2,1,0:T(8,128)}), f32[8,1,16,128]{3,2,1,0:T(8,128)S(1)}, u32[]{:S(2)}, u32[]{:S(2)}) async-start(f32[8,1,16,128]{3,2,1,0:T(8,128)} %coarse_half_1.1), calls=%async_computation.1 | async-start | bytes 131072 | tf_op jit(solution)/shard_map/all_to_all | solution.py:343
  40.1 1.9 %collective-permute-start.1 = (f32[8,128]{1,0:T(8,128)}, f32[8,128]{1,0:T(8,128)S(1)}, u32[]{:S(2)}, u32[]{:S(2)}) collective-permute-start(f32[8,128]{1,0:T(8,128)} %pack_tracks.1.refs_0_), channel_id=1, source_target_pairs={{0,1},{1,0},{2,3},{3,2},{4,5},{5,4},{6,7},{7,6},{8,9},{9,8},{10,11... | collective-permute-start | bytes 12296 | tf_op jit(solution)/shard_map/ppermute | solution.py:328
  40.3 3.8 %collective-permute-start.2 = (f32[8,128]{1,0:T(8,128)}, f32[8,128]{1,0:T(8,128)S(1)}, u32[]{:S(2)}, u32[]{:S(2)}) collective-permute-start(f32[8,128]{1,0:T(8,128)} %pack_tracks.1.refs_0_), channel_id=1, source_target_pairs={{0,2},{1,3},{2,0},{3,1},{4,6},{5,7},{6,4},{7,5},{8,10},{9,11},{10,... | collective-permute-start | bytes 12296 | tf_op jit(solution)/shard_map/ppermute | solution.py:328
  41.8 3.2 %collective-permute-start.3 = (f32[8,128]{1,0:T(8,128)}, f32[8,128]{1,0:T(8,128)S(1)}, u32[]{:S(2)}, u32[]{:S(2)}) collective-permute-start(f32[8,128]{1,0:T(8,128)} %pack_tracks.1.refs_0_), channel_id=1, source_target_pairs={{0,3},{1,2},{2,1},{3,0},{4,7},{5,6},{6,5},{7,4},{8,11},{9,10},{10,... | collective-permute-start | bytes 12296 | tf_op jit(solution)/shard_map/ppermute | solution.py:328
  42.0 3.1 %copy-start.7 = (f32[8,128]{1,0:T(8,128)}, f32[8,128]{1,0:T(8,128)S(1)}, u32[]{:S(2)}) copy-start(f32[8,128]{1,0:T(8,128)S(1)} %collective-permute-done.1.refs_1_) | copy-start | bytes 12292
  44.1 0.9 %copy-start.8 = (f32[8,128]{1,0:T(8,128)}, f32[8,128]{1,0:T(8,128)S(1)}, u32[]{:S(2)}) copy-start(f32[8,128]{1,0:T(8,128)S(1)} %collective-permute-done.2.refs_2_) | copy-start | bytes 12292
  45.0 0.6 %copy-start.9 = (f32[8,128]{1,0:T(8,128)}, f32[8,128]{1,0:T(8,128)S(1)}, u32[]{:S(2)}) copy-start(f32[8,128]{1,0:T(8,128)S(1)} %collective-permute-done.3.refs_3_) | copy-start | bytes 12292
  49.6 1.9 %collective-permute-start.4 = (f32[2,4,2]{2,1,0:T(4,128)}, f32[2,4,2]{2,1,0:T(4,128)S(1)}, u32[]{:S(2)}, u32[]{:S(2)}) collective-permute-start(f32[2,4,2]{2,1,0:T(4,128)} %get-tuple-element.7), channel_id=1, source_target_pairs={{0,1},{1,0},{2,3},{3,2},{4,5},{5,4},{6,7},{7,6},{8,9},{9,8},{10,11... | collective-permute-start | bytes 200 | tf_op jit(solution)/shard_map/ppermute | solution.py:328
  49.8 3.8 %collective-permute-start.5 = (f32[2,4,2]{2,1,0:T(4,128)}, f32[2,4,2]{2,1,0:T(4,128)S(1)}, u32[]{:S(2)}, u32[]{:S(2)}) collective-permute-start(f32[2,4,2]{2,1,0:T(4,128)} %get-tuple-element.8), channel_id=1, source_target_pairs={{0,2},{1,3},{2,0},{3,1},{4,6},{5,7},{6,4},{7,5},{8,10},{9,11},{10,... | collective-permute-start | bytes 200 | tf_op jit(solution)/shard_map/ppermute | solution.py:328
  50.9 3.2 %collective-permute-start.6 = (f32[2,4,2]{2,1,0:T(4,128)}, f32[2,4,2]{2,1,0:T(4,128)S(1)}, u32[]{:S(2)}, u32[]{:S(2)}) collective-permute-start(f32[2,4,2]{2,1,0:T(4,128)} %get-tuple-element.9), channel_id=1, source_target_pairs={{0,3},{1,2},{2,1},{3,0},{4,7},{5,6},{6,5},{7,4},{8,11},{9,10},{10,... | collective-permute-start | bytes 200 | tf_op jit(solution)/shard_map/ppermute | solution.py:328
  51.5 2.6 %copy-start.4 = (f32[2,4,2]{2,1,0:T(4,128)}, f32[2,4,2]{2,1,0:T(4,128)S(1)}, u32[]{:S(2)}) copy-start(f32[2,4,2]{2,1,0:T(4,128)S(1)} %collective-permute-done.4.refs_1_) | copy-start | bytes 196
  53.6 0.6 %copy-start.5 = (f32[2,4,2]{2,1,0:T(4,128)}, f32[2,4,2]{2,1,0:T(4,128)S(1)}, u32[]{:S(2)}) copy-start(f32[2,4,2]{2,1,0:T(4,128)S(1)} %collective-permute-done.5.refs_2_) | copy-start | bytes 196
  54.1 0.6 %copy-start.6 = (f32[2,4,2]{2,1,0:T(4,128)}, f32[2,4,2]{2,1,0:T(4,128)S(1)}, u32[]{:S(2)}) copy-start(f32[2,4,2]{2,1,0:T(4,128)S(1)} %collective-permute-done.6.refs_3_) | copy-start | bytes 196
  54.1 0.6 %copy-start.2 = (f32[8,1,16,128]{3,2,1,0:T(8,128)}, f32[8,1,16,128]{3,2,1,0:T(8,128)S(1)}, u32[]{:S(2)}) copy-start(f32[8,1,16,128]{3,2,1,0:T(8,128)S(1)} %all-to-all-done.1.stats_ref) | copy-start | bytes 196612

commit v2 on v1

v2 whole, which is shorter than its diff:
```python
import functools
import math

import jax
import jax.numpy as jnp
from jax import lax
from jax.experimental import pallas as pl
from jax.experimental.pallas import tpu as pltpu
from jax.sharding import PartitionSpec as P


GH = 68
GW = 120
TILE = 8
LOW = -3e38
spread_cells = 32.0

VMEM = pl.BlockSpec(memory_space=pltpu.VMEM)
SMEM = pl.BlockSpec(memory_space=pltpu.SMEM)
ANY = pl.BlockSpec(memory_space=pl.ANY)
SMALL = pltpu.CompilerParams(vmem_limit_bytes=8 << 20)
LARGE = pltpu.CompilerParams(vmem_limit_bytes=16 << 20)


def pack_kernel(query_ref, pos_ref, out_ref):
    tracks = query_ref.shape[0]
    window = pos_ref.shape[2]
    out_ref[...] = jnp.zeros(out_ref.shape, jnp.float32)
    out_ref[0:tracks, :] = query_ref[...].astype(jnp.float32)
    for k in range(2):
        out_ref[(k + 1) * tracks : (k + 2) * tracks, 0:window] = pos_ref[k].astype(jnp.float32)


def pack_tracks(fine_query, places):
    return pl.pallas_call(
        pack_kernel,
        out_shape=jax.ShapeDtypeStruct((8, fine_query.shape[1]), jnp.float32),
        in_specs=[VMEM, VMEM],
        out_specs=VMEM,
        compiler_params=SMALL,
        name="pack_tracks",
    )(fine_query, places)


def fine_kernel(pieces, own, region, ids_ref, list_ref, valid_ref, tiles_ref, *refs):
    ins, outs = refs[:pieces], refs[pieces:]
    frames, _, cells, channels = tiles_ref.shape
    slots = list_ref.shape[3]
    tracks = pieces * own
    wide = slots * cells
    base = lax.axis_index("blk") * region
    me = lax.axis_index("frames")
    window = outs[0].shape[2]
    scale = 1.0 / math.sqrt(channels)
    query = jnp.concatenate([r[0:own, :] for r in ins], axis=0).astype(jnp.bfloat16)
    rows_in = jnp.concatenate([r[own : 2 * own, :] for r in ins], axis=0)
    cols_in = jnp.concatenate([r[2 * own : 3 * own, :] for r in ins], axis=0)
    lane_in = lax.broadcasted_iota(jnp.int32, (tracks, channels), 1)
    spread = (
        lax.broadcasted_iota(jnp.int32, (slots, wide), 0)
        == lax.broadcasted_iota(jnp.int32, (slots, wide), 1) // cells
    ).astype(jnp.bfloat16)
    inner = lax.broadcasted_iota(jnp.int32, (tracks, wide), 1) % cells
    inner_row = (inner // TILE).astype(jnp.float32)
    inner_col = (inner % TILE).astype(jnp.float32)
    piece_wide = lax.broadcasted_iota(jnp.int32, (tracks, wide), 0) // own
    piece_slot = lax.broadcasted_iota(jnp.int32, (tracks, slots), 0) // own
    lane_out = lax.broadcasted_iota(jnp.int32, (tracks, window), 1)
    rows_out = jnp.zeros((tracks, window), jnp.float32)
    cols_out = jnp.zeros((tracks, window), jnp.float32)
    for i in range(frames):
        scores = jnp.zeros((tracks, wide), jnp.float32)
        codes = jnp.zeros((tracks, slots), jnp.float32)
        for j in range(pieces):
            owner = lax.bitwise_xor(me, j)
            block = jnp.concatenate(
                [tiles_ref[i, ids_ref[i, 0, owner, s]] for s in range(slots)], axis=0
            )
            got = lax.dot_general(
                query, block, (((1,), (1,)), ((), ())), preferred_element_type=jnp.float32
            )
            scores = jnp.where(piece_wide == j, got, scores)
            ids = list_ref[i, 0, pl.ds(owner, 1), :]
            live = valid_ref[i, 0, pl.ds(owner, 1), :]
            code = jnp.where(live > 0, ids, -1).astype(jnp.float32)
            codes = jnp.where(piece_slot == j, jnp.broadcast_to(code, (tracks, slots)), codes)
        code = lax.dot_general(
            codes.astype(jnp.bfloat16),
            spread,
            (((1,), (0,)), ((), ())),
            preferred_element_type=jnp.float32,
        )
        cell = code + base.astype(jnp.float32)
        tile_row = jnp.floor((cell + 0.5) * (1.0 / GW))
        tile_col = cell - GW * tile_row
        here = lane_in == me * frames + i
        track_row = jnp.sum(jnp.where(here, rows_in, 0.0), axis=1, keepdims=True)
        track_col = jnp.sum(jnp.where(here, cols_in, 0.0), axis=1, keepdims=True)
        off_row = (tile_row * TILE + inner_row) - track_row
        off_col = (tile_col * TILE + inner_col) - track_col
        distance = off_row * off_row + off_col * off_col
        scores = scores * scale - distance * (0.5 / (spread_cells * spread_cells))
        scores = jnp.where(code < -0.5, -1e30, scores)
        highest = jnp.max(scores, axis=1, keepdims=True)
        weights = jnp.exp(scores - highest)
        norm = 1.0 / (jnp.sum(weights, axis=1, keepdims=True) * spread_cells)
        mean_row = jnp.sum(weights * off_row, axis=1, keepdims=True) * norm
        mean_col = jnp.sum(weights * off_col, axis=1, keepdims=True) * norm
        rows_out = jnp.where(lane_out == me * frames + i, mean_row, rows_out)
        cols_out = jnp.where(lane_out == me * frames + i, mean_col, cols_out)
    for j in range(pieces):
        outs[j][0] = rows_out[j * own : (j + 1) * own]
        outs[j][1] = cols_out[j * own : (j + 1) * own]


def fine_part(tile_list, tile_valid, fine_tiles, own, window, region, payloads):
    pieces = len(payloads)
    return pl.pallas_call(
        functools.partial(fine_kernel, pieces, own, region),
        out_shape=[jax.ShapeDtypeStruct((2, own, window), jnp.float32)] * pieces,
        in_specs=[SMEM, VMEM, VMEM, VMEM] + [VMEM] * pieces,
        out_specs=[VMEM] * pieces,
        compiler_params=LARGE,
        name="fine_part",
    )(tile_list, tile_list, tile_valid, fine_tiles, *payloads)


def coarse_kernel(half, q_ref, f_ref, gate_ref, *rest):
    if half:
        prev_ref, o_ref, s_ref = rest
    else:
        o_ref, s_ref = rest
    region, frames, channels = f_ref.shape
    groups, rows, _ = q_ref.shape
    per = 256 // rows
    quads = groups // per
    cells = 8 // frames
    run = 15
    seg = run * cells
    factor = math.log2(math.e) / math.sqrt(channels)
    base = lax.axis_index("blk") * region
    sub = lax.broadcasted_iota(jnp.int32, (8, 128), 0)
    inside = (sub // frames).astype(jnp.float32)
    width = min(rows, 128)

    def fold(x):
        y = x
        for k in range(1, cells):
            y = y + pltpu.roll(x, k * frames, 0)
        return y

    def score(quad, at, n):
        q = q_ref[pl.ds(quad * per, per)].reshape(256, channels)
        block = f_ref[pl.ds(at, n)].reshape(n * frames, channels)
        return lax.dot_general(
            block, q, (((1,), (1,)), ((), ())), preferred_element_type=jnp.float32
        )

    def gather(d, at, n, tops, sums):
        out = []
        for lt in range(2):
            total, ramp, row_sum, col_sum = sums[lt]
            for k in range(n // seg):
                acc = None
                for j in range(run):
                    i = k * run + j
                    x = d[8 * i : 8 * i + 8, lt * 128 : (lt + 1) * 128]
                    if tops is not None:
                        x = x - tops[lt]
                    p = jnp.exp2(x * factor)
                    acc = p if acc is None else acc + p
                    ramp = ramp + acc
                first = base + (at + k * seg)
                row = first // GW
                col = first - row * GW
                total = total + acc
                row_sum = row_sum + acc * (row.astype(jnp.float32) - (GH - 1) / 2.0)
                col_sum = col_sum + acc * (col.astype(jnp.float32) - (GW - 1) / 2.0)
            out.append((total, ramp, row_sum, col_sum))
        return out

    zero = jnp.zeros((8, 128), jnp.float32)

    def store(quad, lt, top, sums):
        total, ramp, row_sum, col_sum = sums
        col_sum = col_sum + (run * total - ramp) * float(cells) + total * inside
        total = fold(total)
        for k in range(128 // width):
            column = lt * 128 + k * width
            group = quad * per + column // rows
            lane = half * rows + column % rows
            for st, v in enumerate((top, total, fold(row_sum), fold(col_sum))):
                o_ref[
                    group, lane // 128, st * frames : (st + 1) * frames, lane % 128 : lane % 128 + width
                ] = v[0:frames, k * width : (k + 1) * width]
        return total

    if half:
        if rows < 128:
            o_ref[:, :, :, 0:rows] = prev_ref[:, :, :, 0:rows]
        else:
            o_ref[:, 0 : rows // 128] = prev_ref[:, 0 : rows // 128]

    def plain(quad, worst):
        sums = [(zero, zero, zero, zero)] * 2
        for at in range(0, region, 4 * run):
            n = min(4 * run, region - at)
            sums = gather(score(quad, at, n), at, n, None, sums)
        for lt in range(2):
            total = store(quad, lt, zero, sums[lt])
            good = (total >= 2.0**-90) & (total <= 2.0**100)
            worst = jnp.maximum(worst, jnp.where(good, 0.0, 1.0))
        return worst

    worst = lax.fori_loop(0, quads, plain, zero)

    @pl.when(jnp.max(worst) > 0.0)
    def _():
        chunks = region // seg

        def careful(quad, carry):
            def first(c, best):
                d = score(quad, c * seg, seg)
                s_ref[c] = d
                return jnp.maximum(best, jnp.max(d.reshape(run, 8, 256), axis=0))

            best = lax.fori_loop(0, chunks, first, jnp.full((8, 256), LOW, jnp.float32))
            tops = []
            for lt in range(2):
                top = best[:, lt * 128 : (lt + 1) * 128]
                full = top
                for k in range(1, cells):
                    full = jnp.maximum(full, pltpu.roll(top, k * frames, 0))
                tops.append(full)

            def second(c, sums):
                return gather(s_ref[c], c * seg, seg, tops, sums)

            sums = lax.fori_loop(0, chunks, second, [(zero, zero, zero, zero)] * 2)
            for lt in range(2):
                store(quad, lt, tops[lt], sums[lt])
            return carry

        lax.fori_loop(0, quads, careful, 0)


def coarse_half(q, f, gate, prev=None):
    region, frames, _ = f.shape
    groups, rows, _ = q.shape
    half = 0 if prev is None else 1
    seg = 15 * (8 // frames)
    return pl.pallas_call(
        functools.partial(coarse_kernel, half),
        out_shape=jax.ShapeDtypeStruct((groups, rows // 64, 4 * frames, 128), jnp.float32),
        in_specs=[VMEM, VMEM, ANY] + [VMEM] * half,
        out_specs=VMEM,
        scratch_shapes=[pltpu.VMEM((region // seg, seg * frames, 256), jnp.float32)],
        compiler_params=LARGE,
    )(q, f, gate, *([prev] if half else []))


def finish_kernel(pieces, heads, channels, stats_ref, *refs):
    scale = math.log2(math.e) / math.sqrt(channels)
    ins, (coarse_ref, fine_ref) = refs[:pieces], refs[pieces:]
    me = lax.axis_index("frames")
    sources, tiles, quarter, _ = stats_ref.shape
    frames = quarter // 4
    rows = tiles * 128
    tracks = rows // heads

    def take(d, st):
        return jnp.concatenate(
            [stats_ref[d, t, st * frames : (st + 1) * frames, :] for t in range(tiles)], axis=1
        )

    top = take(0, 0)
    for d in range(1, sources):
        top = jnp.maximum(top, take(d, 0))
    total = jnp.zeros((frames, rows), jnp.float32)
    row = jnp.zeros((frames, rows), jnp.float32)
    col = jnp.zeros((frames, rows), jnp.float32)
    for d in range(sources):
        keep = jnp.exp2((take(d, 0) - top) * scale)
        total = total + take(d, 1) * keep
        row = row + take(d, 2) * keep
        col = col + take(d, 3) * keep
    core = lax.rem(me, 2)
    lane = lax.broadcasted_iota(jnp.int32, (rows, tracks), 0) // heads
    where = lax.broadcasted_iota(jnp.int32, (rows, tracks), 1)
    lane = jnp.where(lane < tracks // 2, lane + core * (tracks // 2), lane - core * (tracks // 2))
    mean = (lane == where).astype(jnp.float32)
    for k, (v, size) in enumerate(((row, GH), (col, GW))):
        coarse_ref[k] = lax.dot_general(
            v / total,
            mean,
            (((1,), (0,)), ((), ())),
            precision=lax.Precision.HIGHEST,
            preferred_element_type=jnp.float32,
        ) * (4.0 / (heads * size))
    for k in range(2):
        fine = ins[0][k]
        for j in range(1, pieces):
            fine = fine + ins[j][k]
        fine_ref[k] = fine


def finish(stats, pieces, heads, channels):
    quarter = stats.shape[2]
    rows = stats.shape[1] * 128
    return pl.pallas_call(
        functools.partial(finish_kernel, len(pieces), heads, channels),
        out_shape=[
            jax.ShapeDtypeStruct((2, quarter // 4, rows // heads), jnp.float32),
            jax.ShapeDtypeStruct(pieces[0].shape, jnp.float32),
        ],
        in_specs=[VMEM] * (1 + len(pieces)),
        out_specs=[VMEM, VMEM],
        compiler_params=SMALL,
        name="finish",
    )(stats, *pieces)


def body(coarse_query, coarse_feat, fine_query, fine_tiles, track_pos, tile_list, tile_valid):
    tracks, heads, channels = coarse_query.shape
    blocks = lax.axis_size("blk")
    owners = lax.axis_size("frames")
    region = coarse_feat.shape[1]
    window = track_pos.shape[1]
    own = fine_query.shape[0]
    me = lax.axis_index("frames").astype(jnp.int32)

    def swap(x, j):
        return lax.ppermute(x, "frames", [(i, i ^ j) for i in range(owners)])

    halves = coarse_query.reshape(2, tracks * heads // 2, channels)
    mine = lax.dynamic_index_in_dim(halves, lax.rem(me, 2), 0, keepdims=True)
    mine = jnp.broadcast_to(mine, (blocks,) + mine.shape[1:])
    first = lax.all_to_all(mine, "blk", split_axis=0, concat_axis=0, tiled=True)

    payload = pack_tracks(fine_query, jnp.transpose(track_pos, (0, 2, 1)))
    payloads = [payload] + [swap(payload, j) for j in range(1, owners)]
    fine = fine_part(tile_list, tile_valid, fine_tiles, own, window, region, payloads)
    gate = fine[0]
    fine = [fine[0]] + [swap(fine[j], j) for j in range(1, owners)]

    cells = jnp.transpose(coarse_feat, (1, 0, 2))
    second = swap(first, 1)
    stats = coarse_half(first, cells, gate)
    stats = coarse_half(second, cells, gate, stats)
    stats = lax.all_to_all(stats, "blk", split_axis=0, concat_axis=0, tiled=True)
    coarse_pos, fine_offset = finish(stats, fine, heads, channels)
    return coarse_pos, jnp.transpose(fine_offset, (0, 2, 1))


def solution(mesh):
    return jax.shard_map(
        body,
        mesh=mesh,
        in_specs=(
            P("blk", None, None),
            P("frames", "blk", None),
            P(("blk", "frames"), None),
            P("frames", "blk", None, None),
            P(None, None, ("blk", "frames")),
            P("frames", "blk", None, None),
            P("frames", "blk", None, None),
        ),
        out_specs=(P(None, "frames", "blk"), P(None, None, ("blk", "frames"))),
        check_vma=False,
    )
```

time: 58.4 us -> 78 us (1.34)
  starting transfers between devices: 7.33 us -> 23.7 us
  Pallas kernels: 19.4 us -> 23.4 us
  waiting for transfers between devices: 5.67 us -> 8.07 us
  local copies, waits for them, and re-layouts: 8.14 us -> 5.76 us
    all_to_all x1, starting transfers between devices: 3.6 us -> 19.8 us  [body(): lax.all_to_all(stats, 'blk', split_axis=0, concat_axis=0, tiled=True)]
    pallas_call x3, Pallas kernels: 16.2 us -> 22.6 us  [the longest x2 21 us: coarse_half(): pl.pallas_call(functools.partial(coarse_kernel, half), out_shape=jax.Shap...]
    all_to_all x1, waiting for transfers between devices: 0.01 us -> 3.22 us  [body(): lax.all_to_all(stats, 'blk', split_axis=0, concat_axis=0, tiled=True)]
    pallas_call x1, Pallas kernels: 1.54 us -> 0.01 us  [pack_tracks(): pl.pallas_call(pack_kernel, out_shape=jax.ShapeDtypeStruct((8, fine_query...]
    pallas_call x1 -> x0, local copies, waits for them, and re-layouts: 1.37 us -> none  [finish(): pl.pallas_call(functools.partial(finish_kernel, len(pieces), heads, chann...]
    unnamed x24 -> x14, local copies, waits for them, and re-layouts: 6.74 us -> 5.74 us
    pallas_call x1, Pallas kernels: 1.7 us -> 0.83 us  [finish(): pl.pallas_call(functools.partial(finish_kernel, len(pieces), heads, chann...]
    ppermute x7, waiting for transfers between devices: 5.67 us -> 4.85 us  [swap(): return lax.ppermute(x, 'frames', [(i, i ^ j) for i in range(owners)])]
  transfers between devices with their start and end apart: 8 -> 8, of which waited for: 4 -> 4; matrix products, arithmetic and copies ran while one was open for 8% -> 0% of each run, Pallas kernels for 20% -> 26%
where the time goes in v2:
time: 78 us; the launch traced here: 77.6 us
  starting transfers between devices  23.7 us (30%)
  Pallas kernels  23.4 us (30%)
  blocking collectives  16 us (21%)
  waiting for transfers between devices  8.07 us (10%)
  local copies, waits for them, and re-layouts  5.76 us (7%)
    pallas_call x2, Pallas kernels, coarse_half(): pl.pallas_call(functools.partial(coarse_kernel, half), out_shape=jax.Shap...  21 us
    all_to_all x1, starting transfers between devices, body(): lax.all_to_all(stats, 'blk', split_axis=0, concat_axis=0, tiled=True)  19.8 us
    all_to_all x1, blocking collectives, body(): first = lax.all_to_all(mine, 'blk', split_axis=0, concat_axis=0, tiled=True)  16 us
    unnamed x14, local copies, waits for them, and re-layouts  5.74 us
    ppermute x7, waiting for transfers between devices, swap(): return lax.ppermute(x, 'frames', [(i, i ^ j) for i in range(owners)])  4.85 us
    ppermute x7, starting transfers between devices, swap(): return lax.ppermute(x, 'frames', [(i, i ^ j) for i in range(owners)])  3.86 us
    all_to_all x1, waiting for transfers between devices, body(): lax.all_to_all(stats, 'blk', split_axis=0, concat_axis=0, tiled=True)  3.22 us
    pallas_call x1, Pallas kernels, fine_part(): pl.pallas_call(functools.partial(fine_kernel, pieces, own, region), out_s...  1.57 us
  transfers between devices with their start and end apart: 8, of which 4 were waited for; matrix products, arithmetic and copies ran while one was open for 0% of the time, Pallas kernels for 26%

profile of v2, /device:TPU:0, one launch (start us, length us, event | category | flops | bytes accessed | tf_op | source)
XLA Modules:
  0.0 77.6 jit_solution(17553450314950021865)
XLA Ops:
  0.6 0.0 copy-start
  0.7 0.8 %copy-done = bf16[8,16,256]{2,1,0:T(8,128)(2,1)S(1)} copy-done((bf16[8,16,256]{2,1,0:T(8,128)(2,1)S(1)}, bf16[8,16,256]{2,1,0:T(8,128)(2,1)}, u32[]{:S(2)}) %copy-start) | copy-done | bytes 65560
  1.5 16.0 %all_to_all.10.q_ref = bf16[8,64,256]{2,1,0:T(8,128)(2,1)S(1)} all-to-all(bf16[8,64,256]{2,1,0:T(8,128)(2,1)S(1)} %broadcast_in_dim.8), channel_id=1, replica_groups=mesh['blk'=8,'frames'=4] {'blk'}, dimensions={0} | all-to-all | bytes 524288 | tf_op jit(solution)/shard_map/all_to_all | solution.py:338
  17.5 0.7 copy-done.5
  18.2 0.7 copy-done.6
  18.9 0.5 collective-permute-start.1
  19.4 1.5 %collective-permute-start.2 = (f32[8,128]{1,0:T(8,128)S(1)}, f32[8,128]{1,0:T(8,128)S(1)}, u32[]{:S(2)}, u32[]{:S(2)}) collective-permute-start(f32[8,128]{1,0:T(8,128)S(1)} %pack_tracks.1.refs_0_), channel_id=1, source_target_pairs={{0,2},{1,3},{2,0},{3,1},{4,6},{5,7},{6,4},{7,5},{8,10},{9,11},{10,... | collective-permute-start | bytes 12296 | tf_op jit(solution)/shard_map/ppermute | solution.py:333
  20.9 2.1 %collective-permute-done.2.refs_2_ = f32[8,128]{1,0:T(8,128)S(1)} collective-permute-done((f32[8,128]{1,0:T(8,128)S(1)}, f32[8,128]{1,0:T(8,128)S(1)}, u32[]{:S(2)}, u32[]{:S(2)}) %collective-permute-start.2) | collective-permute-done | bytes 4128 | tf_op jit(solution)/shard_map/ppermute | solution.py:333
  23.0 0.9 %collective-permute-done.3.refs_3_ = f32[8,128]{1,0:T(8,128)S(1)} collective-permute-done((f32[8,128]{1,0:T(8,128)S(1)}, f32[8,128]{1,0:T(8,128)S(1)}, u32[]{:S(2)}, u32[]{:S(2)}) %collective-permute-start.3) | collective-permute-done | bytes 4128 | tf_op jit(solution)/shard_map/ppermute | solution.py:333
  23.9 2.2 %copy-done.2 = bf16[4,64,64,128]{3,2,1,0:T(8,128)(2,1)S(1)} copy-done((bf16[4,64,64,128]{3,2,1,0:T(8,128)(2,1)S(1)}, bf16[4,64,64,128]{3,2,1,0:T(8,128)(2,1)}, u32[]{:S(2)}) %copy-start.2) | copy-done | bytes 4194328
  26.1 0.7 copy-done.3
  26.8 0.7 copy-done.4
  27.5 1.6 %fine_part.1 = (f32[2,2,16]{2,1,0:T(2,128)S(1)}, f32[2,2,16]{2,1,0:T(2,128)S(1)}, f32[2,2,16]{2,1,0:T(2,128)S(1)}, f32[2,2,16]{2,1,0:T(2,128)S(1)}) custom-call(s32[4,1,4,8]{3,2,1,0:T(4,128)S(1)} %copy-done.3, s32[4,1,4,8]{3,2,1,0:T(4,128)S(1)} %copy-done.3, s32[4,1,4,8]{3,2,1,0:T(4,128)S(1)} %copy-done.4, bf16[4,64,64,128]{3,2,1,0:T(8,128)(2,1)S(1)} %copy-done.2, ...), custom_call_target="tpu_custom_call" | custom-call | tf_op jit(solution)/shard_map/fine_part/pallas_call | solution.py:118
  29.1 18.3 %shard_map.86.rest_0_ = f32[8,1,16,128]{3,2,1,0:T(8,128)S(1)} custom-call(bf16[8,64,256]{2,1,0:T(8,128)(2,1)S(1)} %all_to_all.10.q_ref, bf16[1020,4,256]{2,1,0:T(4,128)(2,1)S(1)} %bitcast.7, f32[2,2,16]{2,1,0:T(2,128)S(1)} %get-tuple-element.8.gate_ref.refs_0_), custom_call_target="tpu_custom_call" | custom-call | tf_op jit(solution)/shard_map/pallas_call | solution.py:252
  47.3 0.0 collective-permute-done.q_ref
  47.3 2.7 %shard_map.87 = f32[8,1,16,128]{3,2,1,0:T(8,128)} custom-call(bf16[8,64,256]{2,1,0:T(8,128)(2,1)S(1)} %collective-permute-done.q_ref, bf16[1020,4,256]{2,1,0:T(4,128)(2,1)S(1)} %bitcast.8, f32[2,2,16]{2,1,0:T(2,128)S(1)} %get-tuple-element.8.gate_ref.refs_0_, f32[8,1,16,128]{3,2,1,0:T(8,128)S(1)} %shard_map.86.rest_0_), custom_call_target="tpu_custom_call" | custom-call | tf_op jit(solution)/shard_map/pallas_call | solution.py:252
  50.1 19.8 %all-to-all-start.1 = ((f32[8,1,16,128]{3,2,1,0:T(8,128)}), f32[8,1,16,128]{3,2,1,0:T(8,128)S(1)}, u32[]{:S(2)}, u32[]{:S(2)}) async-start(f32[8,1,16,128]{3,2,1,0:T(8,128)} %shard_map.87), calls=%async_computation.1 | async-start | bytes 131072 | tf_op jit(solution)/shard_map/all_to_all | solution.py:350
  69.9 0.0 collective-permute-start.4
  69.9 0.6 collective-permute-start.5
  70.6 1.2 %collective-permute-start.6 = (f32[2,2,16]{2,1,0:T(2,128)S(1)}, f32[2,2,16]{2,1,0:T(2,128)S(1)}, u32[]{:S(2)}, u32[]{:S(2)}) collective-permute-start(f32[2,2,16]{2,1,0:T(2,128)S(1)} %get-tuple-element.11), channel_id=1, source_target_pairs={{0,3},{1,2},{2,1},{3,0},{4,7},{5,6},{6,5},{7,4},{8,11},{9,10},{10,... | collective-permute-start | bytes 776 | tf_op jit(solution)/shard_map/ppermute | solution.py:333
  71.8 1.8 %collective-permute-done.5.refs_2_ = f32[2,2,16]{2,1,0:T(2,128)S(1)} collective-permute-done((f32[2,2,16]{2,1,0:T(2,128)S(1)}, f32[2,2,16]{2,1,0:T(2,128)S(1)}, u32[]{:S(2)}, u32[]{:S(2)}) %collective-permute-start.5) | collective-permute-done | bytes 288 | tf_op jit(solution)/shard_map/ppermute | solution.py:333
  73.6 0.0 collective-permute-done.6.refs_3_
  73.6 3.2 %all-to-all-done.1.stats_ref = f32[8,1,16,128]{3,2,1,0:T(8,128)S(1)} async-done(((f32[8,1,16,128]{3,2,1,0:T(8,128)}), f32[8,1,16,128]{3,2,1,0:T(8,128)S(1)}, u32[]{:S(2)}, u32[]{:S(2)}) %all-to-all-start.1) | async-done | bytes 65568 | tf_op jit(solution)/shard_map/all_to_all | solution.py:350
  76.8 0.8 %finish.1 = (f32[2,4,8]{2,1,0:T(4,128)}, f32[2,2,16]{2,1,0:T(2,128)}) custom-call(f32[8,1,16,128]{3,2,1,0:T(8,128)S(1)} %all-to-all-done.1.stats_ref, f32[2,2,16]{2,1,0:T(2,128)S(1)} %get-tuple-element.8.gate_ref.refs_0_, f32[2,2,16]{2,1,0:T(2,128)S(1)} %collective-permute-done.4.refs_1_, f32[2,2,16]{2,1,0:T(2,128)S(1)} %collective-permute-done.5.refs_2_, ...), custom_call_target="tpu_custom_call" | custom-call | tf_op jit(solution)/shard_map/finish/pallas_call | solution.py:310
  (14 shorter events, 0.0 us)
Async XLA Ops:
  0.6 0.8 %copy-start = (bf16[8,16,256]{2,1,0:T(8,128)(2,1)S(1)}, bf16[8,16,256]{2,1,0:T(8,128)(2,1)}, u32[]{:S(2)}) copy-start(bf16[8,16,256]{2,1,0:T(8,128)(2,1)} %param.7) | copy-start | bytes 196612
  0.6 28.4 %copy-start.1 = (bf16[4,1020,256]{2,0,1:T(4,128)(2,1)S(1)}, bf16[4,1020,256]{2,0,1:T(4,128)(2,1)}, u32[]{:S(2)}) copy-start(bf16[4,1020,256]{2,0,1:T(4,128)(2,1)} %param.8) | copy-start | bytes 6266884
  17.5 29.8 %collective-permute-start = (bf16[8,64,256]{2,1,0:T(8,128)(2,1)S(1)}, bf16[8,64,256]{2,1,0:T(8,128)(2,1)S(1)}, u32[]{:S(2)}, u32[]{:S(2)}) collective-permute-start(bf16[8,64,256]{2,1,0:T(8,128)(2,1)S(1)} %all_to_all.10.q_ref), channel_id=1, source_target_pairs={{0,1},{1,0},{2,3},{3,2},{4,5},{5,4},{6,7},{7,6},{8,9},{9,8},{10,11... | collective-permute-start | bytes 786440 | tf_op jit(solution)/shard_map/ppermute | solution.py:333
  17.5 0.7 copy-start.5
  18.2 0.7 copy-start.6
  18.9 2.0 %collective-permute-start.1 = (f32[8,128]{1,0:T(8,128)S(1)}, f32[8,128]{1,0:T(8,128)S(1)}, u32[]{:S(2)}, u32[]{:S(2)}) collective-permute-start(f32[8,128]{1,0:T(8,128)S(1)} %pack_tracks.1.refs_0_), channel_id=1, source_target_pairs={{0,1},{1,0},{2,3},{3,2},{4,5},{5,4},{6,7},{7,6},{8,9},{9,8},{10,11... | collective-permute-start | bytes 12296 | tf_op jit(solution)/shard_map/ppermute | solution.py:333
  19.4 3.6 %collective-permute-start.2 = (f32[8,128]{1,0:T(8,128)S(1)}, f32[8,128]{1,0:T(8,128)S(1)}, u32[]{:S(2)}, u32[]{:S(2)}) collective-permute-start(f32[8,128]{1,0:T(8,128)S(1)} %pack_tracks.1.refs_0_), channel_id=1, source_target_pairs={{0,2},{1,3},{2,0},{3,1},{4,6},{5,7},{6,4},{7,5},{8,10},{9,11},{10,... | collective-permute-start | bytes 12296 | tf_op jit(solution)/shard_map/ppermute | solution.py:333
  20.9 3.0 %collective-permute-start.3 = (f32[8,128]{1,0:T(8,128)S(1)}, f32[8,128]{1,0:T(8,128)S(1)}, u32[]{:S(2)}, u32[]{:S(2)}) collective-permute-start(f32[8,128]{1,0:T(8,128)S(1)} %pack_tracks.1.refs_0_), channel_id=1, source_target_pairs={{0,3},{1,2},{2,1},{3,0},{4,7},{5,6},{6,5},{7,4},{8,11},{9,10},{10,... | collective-permute-start | bytes 12296 | tf_op jit(solution)/shard_map/ppermute | solution.py:333
  23.9 2.2 %copy-start.2 = (bf16[4,64,64,128]{3,2,1,0:T(8,128)(2,1)S(1)}, bf16[4,64,64,128]{3,2,1,0:T(8,128)(2,1)}, u32[]{:S(2)}) copy-start(bf16[4,64,64,128]{3,2,1,0:T(8,128)(2,1)} %tiles_ref.1) | copy-start | bytes 12582916
  26.1 0.7 copy-start.3
  26.8 0.7 copy-start.4
  50.1 26.7 %all-to-all-start.1 = ((f32[8,1,16,128]{3,2,1,0:T(8,128)}), f32[8,1,16,128]{3,2,1,0:T(8,128)S(1)}, u32[]{:S(2)}, u32[]{:S(2)}) async-start(f32[8,1,16,128]{3,2,1,0:T(8,128)} %shard_map.87), calls=%async_computation.1 | async-start | bytes 131072 | tf_op jit(solution)/shard_map/all_to_all | solution.py:350
  69.9 1.9 %collective-permute-start.4 = (f32[2,2,16]{2,1,0:T(2,128)S(1)}, f32[2,2,16]{2,1,0:T(2,128)S(1)}, u32[]{:S(2)}, u32[]{:S(2)}) collective-permute-start(f32[2,2,16]{2,1,0:T(2,128)S(1)} %get-tuple-element.9), channel_id=1, source_target_pairs={{0,1},{1,0},{2,3},{3,2},{4,5},{5,4},{6,7},{7,6},{8,9},{9,8},{10,11... | collective-permute-start | bytes 776 | tf_op jit(solution)/shard_map/ppermute | solution.py:333
  69.9 3.7 %collective-permute-start.5 = (f32[2,2,16]{2,1,0:T(2,128)S(1)}, f32[2,2,16]{2,1,0:T(2,128)S(1)}, u32[]{:S(2)}, u32[]{:S(2)}) collective-permute-start(f32[2,2,16]{2,1,0:T(2,128)S(1)} %get-tuple-element.10), channel_id=1, source_target_pairs={{0,2},{1,3},{2,0},{3,1},{4,6},{5,7},{6,4},{7,5},{8,10},{9,11},{10,... | collective-permute-start | bytes 776 | tf_op jit(solution)/shard_map/ppermute | solution.py:333
  70.6 3.0 %collective-permute-start.6 = (f32[2,2,16]{2,1,0:T(2,128)S(1)}, f32[2,2,16]{2,1,0:T(2,128)S(1)}, u32[]{:S(2)}, u32[]{:S(2)}) collective-permute-start(f32[2,2,16]{2,1,0:T(2,128)S(1)} %get-tuple-element.11), channel_id=1, source_target_pairs={{0,3},{1,2},{2,1},{3,0},{4,7},{5,6},{6,5},{7,4},{8,11},{9,10},{10,... | collective-permute-start | bytes 776 | tf_op jit(solution)/shard_map/ppermute | solution.py:333

commit v3 on v2

--- a/solution.py
+++ b/solution.py
@@ -15,37 +15,117 @@
 LOW = -3e38
 spread_cells = 32.0
 
+
 VMEM = pl.BlockSpec(memory_space=pltpu.VMEM)
 SMEM = pl.BlockSpec(memory_space=pltpu.SMEM)
 ANY = pl.BlockSpec(memory_space=pl.ANY)
+HBM = pl.BlockSpec(memory_space=pltpu.HBM)
 SMALL = pltpu.CompilerParams(vmem_limit_bytes=8 << 20)
 LARGE = pltpu.CompilerParams(vmem_limit_bytes=16 << 20)
 
 
-def pack_kernel(query_ref, pos_ref, out_ref):
-    tracks = query_ref.shape[0]
-    window = pos_ref.shape[2]
-    out_ref[...] = jnp.zeros(out_ref.shape, jnp.float32)
-    out_ref[0:tracks, :] = query_ref[...].astype(jnp.float32)
+def stay(x):
+    return pltpu.with_memory_space_constraint(x, pltpu.HBM)
+
+
+def prepare_kernel(halves_ref, query_ref, pos_ref, mine_ref, pack_ref, half, query, pos, sems):
+    core = lax.rem(lax.axis_index("frames"), 2)
+    copies = [
+        pltpu.make_async_copy(src, dst, sems.at[k])
+        for k, (src, dst) in enumerate(
+            ((halves_ref.at[core], half), (query_ref, query), (pos_ref, pos))
+        )
+    ]
+    for copy in copies:
+        copy.start()
+    for copy in copies:
+        copy.wait()
+    for k in range(mine_ref.shape[0]):
+        mine_ref[k] = half[...]
+    tracks = query.shape[0]
+    window = pos.shape[2]
+    pack_ref[...] = jnp.zeros(pack_ref.shape, jnp.float32)
+    pack_ref[0:tracks, :] = query[...].astype(jnp.float32)
     for k in range(2):
-        out_ref[(k + 1) * tracks : (k + 2) * tracks, 0:window] = pos_ref[k].astype(jnp.float32)
-
-
-def pack_tracks(fine_query, places):
+        pack_ref[(k + 1) * tracks : (k + 2) * tracks, 0:window] = pos[k].astype(jnp.float32)
+
+
+def prepare(blocks, halves, fine_query, places):
+    _, rows, channels = halves.shape
     return pl.pallas_call(
-        pack_kernel,
-        out_shape=jax.ShapeDtypeStruct((8, fine_query.shape[1]), jnp.float32),
-        in_specs=[VMEM, VMEM],
-        out_specs=VMEM,
+        prepare_kernel,
+        out_shape=[
+            jax.ShapeDtypeStruct((blocks, rows, channels), halves.dtype),
+            jax.ShapeDtypeStruct((8, fine_query.shape[1]), jnp.float32),
+        ],
+        in_specs=[HBM] * 3,
+        out_specs=[VMEM] * 2,
+        scratch_shapes=[
+            pltpu.VMEM((rows, channels), halves.dtype),
+            pltpu.VMEM(fine_query.shape, fine_query.dtype),
+            pltpu.VMEM(places.shape, places.dtype),
+            pltpu.SemaphoreType.DMA((3,)),
+        ],
         compiler_params=SMALL,
-        name="pack_tracks",
-    )(fine_query, places)
-
-
-def fine_kernel(pieces, own, region, ids_ref, list_ref, valid_ref, tiles_ref, *refs):
+        name="prepare",
+    )(*(stay(x) for x in (halves, fine_query, places)))
+
+
+def fetch_kernel(pieces, own, ids_ref, list_ref, valid_ref, tiles_ref, out_ref, codes_ref, ids, live, sems):
+    frames, _, slots = out_ref.shape[:3]
+    me = lax.axis_index("frames")
+    copies = [
+        pltpu.make_async_copy(list_ref, ids, sems.at[frames]),
+        pltpu.make_async_copy(valid_ref, live, sems.at[frames + 1]),
+    ]
+    for copy in copies:
+        copy.start()
+    for i in range(frames):
+        for j in range(pieces):
+            for s in range(slots):
+                tile = ids_ref[i, 0, lax.bitwise_xor(me, j), s]
+                pltpu.make_async_copy(
+                    tiles_ref.at[i, tile], out_ref.at[i, j, s], sems.at[i]
+                ).start()
+    for copy in copies:
+        copy.wait()
+    for i in range(frames):
+        for j in range(pieces):
+            owner = lax.bitwise_xor(me, j)
+            code = jnp.where(
+                live[i, 0, pl.ds(owner, 1), :] > 0, ids[i, 0, pl.ds(owner, 1), :], -1
+            ).astype(jnp.float32)
+            for k in range(own):
+                row = (i * pieces + j) * own + k
+                codes_ref[row : row + 1, :] = code
+    for i in range(frames):
+        pltpu.make_async_copy(out_ref.at[i], out_ref.at[i], sems.at[i]).wait()
+
+
+def fetch(tile_list, tile_valid, fine_tiles, pieces, own):
+    frames, _, cells, channels = fine_tiles.shape
+    slots = tile_list.shape[3]
+    return pl.pallas_call(
+        functools.partial(fetch_kernel, pieces, own),
+        out_shape=[
+            jax.ShapeDtypeStruct((frames, pieces, slots, cells, channels), fine_tiles.dtype),
+            jax.ShapeDtypeStruct((frames * pieces * own, slots), jnp.float32),
+        ],
+        in_specs=[SMEM, HBM, HBM, HBM],
+        out_specs=[VMEM] * 2,
+        scratch_shapes=[
+            pltpu.VMEM(tile_list.shape, tile_list.dtype),
+            pltpu.VMEM(tile_valid.shape, tile_valid.dtype),
+            pltpu.SemaphoreType.DMA((frames + 2,)),
+        ],
+        compiler_params=SMALL,
+        name="fetch",
+    )(tile_list, *(stay(x) for x in (tile_list, tile_valid, fine_tiles)))
+
+
+def fine_kernel(pieces, own, region, codes_ref, tiles_ref, *refs):
     ins, outs = refs[:pieces], refs[pieces:]
-    frames, _, cells, channels = tiles_ref.shape
-    slots = list_ref.shape[3]
+    frames, _, slots, cells, channels = tiles_ref.shape
     tracks = pieces * own
     wide = slots * cells
     base = lax.axis_index("blk") * region
@@ -63,33 +143,27 @@
     inner = lax.broadcasted_iota(jnp.int32, (tracks, wide), 1) % cells
     inner_row = (inner // TILE).astype(jnp.float32)
     inner_col = (inner % TILE).astype(jnp.float32)
-    piece_wide = lax.broadcasted_iota(jnp.int32, (tracks, wide), 0) // own
-    piece_slot = lax.broadcasted_iota(jnp.int32, (tracks, slots), 0) // own
+    piece = lax.broadcasted_iota(jnp.int32, (tracks, wide), 0) // own
     lane_out = lax.broadcasted_iota(jnp.int32, (tracks, window), 1)
     rows_out = jnp.zeros((tracks, window), jnp.float32)
     cols_out = jnp.zeros((tracks, window), jnp.float32)
+    codes = lax.dot_general(
+        codes_ref[...].astype(jnp.bfloat16),
+        spread,
+        (((1,), (0,)), ((), ())),
+        preferred_element_type=jnp.float32,
+    )
     for i in range(frames):
-        scores = jnp.zeros((tracks, wide), jnp.float32)
-        codes = jnp.zeros((tracks, slots), jnp.float32)
+        scores = None
         for j in range(pieces):
-            owner = lax.bitwise_xor(me, j)
-            block = jnp.concatenate(
-                [tiles_ref[i, ids_ref[i, 0, owner, s]] for s in range(slots)], axis=0
+            got = lax.dot_general(
+                query,
+                tiles_ref[i, j].reshape(wide, channels),
+                (((1,), (1,)), ((), ())),
+                preferred_element_type=jnp.float32,
             )
-            got = lax.dot_general(
-                query, block, (((1,), (1,)), ((), ())), preferred_element_type=jnp.float32
-            )
-            scores = jnp.where(piece_wide == j, got, scores)
-            ids = list_ref[i, 0, pl.ds(owner, 1), :]
-            live = valid_ref[i, 0, pl.ds(owner, 1), :]
-            code = jnp.where(live > 0, ids, -1).astype(jnp.float32)
-            codes = jnp.where(piece_slot == j, jnp.broadcast_to(code, (tracks, slots)), codes)
-        code = lax.dot_general(
-            codes.astype(jnp.bfloat16),
-            spread,
-            (((1,), (0,)), ((), ())),
-            preferred_element_type=jnp.float32,
-        )
+            scores = got if scores is None else jnp.where(piece == j, got, scores)
+        code = codes[i * tracks : (i + 1) * tracks]
         cell = code + base.astype(jnp.float32)
         tile_row = jnp.floor((cell + 0.5) * (1.0 / GW))
         tile_col = cell - GW * tile_row
@@ -113,16 +187,16 @@
         outs[j][1] = cols_out[j * own : (j + 1) * own]
 
 
-def fine_part(tile_list, tile_valid, fine_tiles, own, window, region, payloads):
+def fine_part(codes, tiles, own, window, region, payloads):
     pieces = len(payloads)
     return pl.pallas_call(
         functools.partial(fine_kernel, pieces, own, region),
         out_shape=[jax.ShapeDtypeStruct((2, own, window), jnp.float32)] * pieces,
-        in_specs=[SMEM, VMEM, VMEM, VMEM] + [VMEM] * pieces,
+        in_specs=[VMEM, VMEM] + [VMEM] * pieces,
         out_specs=[VMEM] * pieces,
-        compiler_params=LARGE,
+        compiler_params=SMALL,
         name="fine_part",
-    )(tile_list, tile_list, tile_valid, fine_tiles, *payloads)
+    )(codes, tiles, *payloads)
 
 
 def coarse_kernel(half, q_ref, f_ref, gate_ref, *rest):
@@ -327,19 +401,16 @@
     region = coarse_feat.shape[1]
     window = track_pos.shape[1]
     own = fine_query.shape[0]
-    me = lax.axis_index("frames").astype(jnp.int32)
 
     def swap(x, j):
         return lax.ppermute(x, "frames", [(i, i ^ j) for i in range(owners)])
 
     halves = coarse_query.reshape(2, tracks * heads // 2, channels)
-    mine = lax.dynamic_index_in_dim(halves, lax.rem(me, 2), 0, keepdims=True)
-    mine = jnp.broadcast_to(mine, (blocks,) + mine.shape[1:])
+    mine, payload = prepare(blocks, halves, fine_query, jnp.transpose(track_pos, (0, 2, 1)))
     first = lax.all_to_all(mine, "blk", split_axis=0, concat_axis=0, tiled=True)
-
-    payload = pack_tracks(fine_query, jnp.transpose(track_pos, (0, 2, 1)))
     payloads = [payload] + [swap(payload, j) for j in range(1, owners)]
-    fine = fine_part(tile_list, tile_valid, fine_tiles, own, window, region, payloads)
+    tiles, codes = fetch(tile_list, tile_valid, fine_tiles, owners, own)
+    fine = fine_part(codes, tiles, own, window, region, payloads)
     gate = fine[0]
     fine = [fine[0]] + [swap(fine[j], j) for j in range(1, owners)]
 

time: 78 us -> 73 us (0.936)
  local copies, waits for them, and re-layouts: 5.76 us -> 0.4 us
  Pallas kernels: 23.4 us -> 26.4 us
  waiting for transfers between devices: 8.07 us -> 5.2 us
    unnamed x14 -> x2, local copies, waits for them, and re-layouts: 5.74 us -> 0.4 us
    pallas_call x1 -> x2, Pallas kernels: 0.01 us -> 3.51 us  [the longest x1 2.69 us: fetch(): pl.pallas_call(functools.partial(fetch_kernel, pieces, own), out_shape=[j...]
    ppermute x7, waiting for transfers between devices: 4.85 us -> 3.27 us  [swap(): return lax.ppermute(x, 'frames', [(i, i ^ j) for i in range(owners)])]
    all_to_all x1, waiting for transfers between devices: 3.22 us -> 1.93 us  [body(): lax.all_to_all(stats, 'blk', split_axis=0, concat_axis=0, tiled=True)]
  transfers between devices with their start and end apart: 8 -> 8, of which waited for: 4 -> 4; matrix products, arithmetic and copies ran while one was open for 0% -> 0% of each run, Pallas kernels for 26% -> 30%
where the time goes in v3:
time: 73 us; the launch traced here: 72.5 us
  Pallas kernels  26.4 us (36%)
  starting transfers between devices  23.7 us (32%)
  blocking collectives  16 us (22%)
  waiting for transfers between devices  5.2 us (7%)
    pallas_call x2, Pallas kernels, coarse_half(): pl.pallas_call(functools.partial(coarse_kernel, half), out_shape=jax.Shap...  21.2 us
    all_to_all x1, starting transfers between devices, body(): lax.all_to_all(stats, 'blk', split_axis=0, concat_axis=0, tiled=True)  19.6 us
    all_to_all x1, blocking collectives, body(): first = lax.all_to_all(mine, 'blk', split_axis=0, concat_axis=0, tiled=True)  16 us
    ppermute x7, starting transfers between devices, swap(): return lax.ppermute(x, 'frames', [(i, i ^ j) for i in range(owners)])  4.11 us
    ppermute x7, waiting for transfers between devices, swap(): return lax.ppermute(x, 'frames', [(i, i ^ j) for i in range(owners)])  3.27 us
    pallas_call x1, Pallas kernels, fetch(): pl.pallas_call(functools.partial(fetch_kernel, pieces, own), out_shape=[j...  2.69 us
    all_to_all x1, waiting for transfers between devices, body(): lax.all_to_all(stats, 'blk', split_axis=0, concat_axis=0, tiled=True)  1.93 us
  transfers between devices with their start and end apart: 8, of which 4 were waited for; matrix products, arithmetic and copies ran while one was open for 0% of the time, Pallas kernels for 30%

profile of v3, /device:TPU:0, one launch (start us, length us, event | category | flops | bytes accessed | tf_op | source)
XLA Modules:
  0.0 72.5 jit_solution(4917985705695877418)
XLA Ops:
  0.6 0.8 %prepare.1 = (bf16[8,64,256]{2,1,0:T(8,128)(2,1)S(1)}, f32[8,128]{1,0:T(8,128)S(1)}) custom-call(bf16[2,64,256]{2,1,0:T(8,128)(2,1)} %bitcast.6, bf16[2,128]{1,0:T(2,128)(2,1)} %query_ref.1, s32[2,2,16]{2,1,0:T(2,128)} %bitcast.7), custom_call_target="tpu_custom_call" | custom-call | tf_op jit(solution)/shard_map/prepare/pallas_call | solution.py:55
  1.5 16.0 %all_to_all.10.q_ref = bf16[8,64,256]{2,1,0:T(8,128)(2,1)S(1)} all-to-all(bf16[8,64,256]{2,1,0:T(8,128)(2,1)S(1)} %get-tuple-element.12), channel_id=1, replica_groups=mesh['blk'=8,'frames'=4] {'blk'}, dimensions={0} | all-to-all | bytes 524288 | tf_op jit(solution)/shard_map/all_to_all | solution.py:410
  17.5 0.0 collective-permute-start
  17.5 0.5 collective-permute-start.1
  18.0 1.5 %collective-permute-start.2 = (f32[8,128]{1,0:T(8,128)S(1)}, f32[8,128]{1,0:T(8,128)S(1)}, u32[]{:S(2)}, u32[]{:S(2)}) collective-permute-start(f32[8,128]{1,0:T(8,128)S(1)} %get-tuple-element.15.refs_0_), channel_id=1, source_target_pairs={{0,2},{1,3},{2,0},{3,1},{4,6},{5,7},{6,4},{7,5},{8,10},{9,11},{10,... | collective-permute-start | bytes 12296 | tf_op jit(solution)/shard_map/ppermute | solution.py:406
  19.5 0.0 collective-permute-start.3
  19.5 2.7 %fetch.1 = (bf16[4,4,8,64,128]{4,3,2,1,0:T(8,128)(2,1)S(1)}, f32[32,8]{1,0:T(8,128)S(1)}) custom-call(s32[4,1,4,8]{3,2,1,0:T(4,128)} %list_ref.1, s32[4,1,4,8]{3,2,1,0:T(4,128)} %list_ref.1, s32[4,1,4,8]{3,2,1,0:T(4,128)} %valid_ref.1, bf16[4,64,64,128]{3,2,1,0:T(8,128)(2,1)} %tiles_ref.1), custom_call_target="tpu_custom_call" | custom-call | tf_op jit(solution)/shard_map/fetch/pallas_call | solution.py:108
  22.2 0.0 copy-start
  22.2 0.0 collective-permute-done.2.refs_2_
  22.2 0.3 collective-permute-done.3.refs_3_
  22.5 0.9 %fine_part.1 = (f32[2,2,16]{2,1,0:T(2,128)S(1)}, f32[2,2,16]{2,1,0:T(2,128)S(1)}, f32[2,2,16]{2,1,0:T(2,128)S(1)}, f32[2,2,16]{2,1,0:T(2,128)S(1)}) custom-call(f32[32,8]{1,0:T(8,128)S(1)} %get-tuple-element.13.codes_ref, bf16[4,4,8,64,128]{4,3,2,1,0:T(8,128)(2,1)S(1)} %get-tuple-element.14.tiles_ref, f32[8,128]{1,0:T(8,128)S(1)} %get-tuple-element.15.refs_0_, ...), custom_call_target="tpu_custom_call" | custom-call | tf_op jit(solution)/shard_map/fine_part/pallas_call | solution.py:192
  23.4 0.4 copy-done
  23.8 18.4 %shard_map.86.rest_0_ = f32[8,1,16,128]{3,2,1,0:T(8,128)S(1)} custom-call(bf16[8,64,256]{2,1,0:T(8,128)(2,1)S(1)} %all_to_all.10.q_ref, bf16[1020,4,256]{2,1,0:T(4,128)(2,1)S(1)} %bitcast.4, f32[2,2,16]{2,1,0:T(2,128)S(1)} %get-tuple-element.16.gate_ref.refs_0_), custom_call_target="tpu_custom_call" | custom-call | tf_op jit(solution)/shard_map/pallas_call | solution.py:326
  42.2 0.0 collective-permute-done.q_ref
  42.2 2.9 %shard_map.87 = f32[8,1,16,128]{3,2,1,0:T(8,128)} custom-call(bf16[8,64,256]{2,1,0:T(8,128)(2,1)S(1)} %collective-permute-done.q_ref, bf16[1020,4,256]{2,1,0:T(4,128)(2,1)S(1)} %bitcast.5, f32[2,2,16]{2,1,0:T(2,128)S(1)} %get-tuple-element.16.gate_ref.refs_0_, f32[8,1,16,128]{3,2,1,0:T(8,128)S(1)} %shard_map.86.rest_0_), custom_call_target="tpu_custom_call" | custom-call | tf_op jit(solution)/shard_map/pallas_call | solution.py:326
  45.0 19.6 %all-to-all-start.1 = ((f32[8,1,16,128]{3,2,1,0:T(8,128)}), f32[8,1,16,128]{3,2,1,0:T(8,128)S(1)}, u32[]{:S(2)}, u32[]{:S(2)}) async-start(f32[8,1,16,128]{3,2,1,0:T(8,128)} %shard_map.87), calls=%async_computation.1 | async-start | bytes 131072 | tf_op jit(solution)/shard_map/all_to_all | solution.py:421
  64.6 0.7 collective-permute-start.4
  65.3 1.4 %collective-permute-start.5 = (f32[2,2,16]{2,1,0:T(2,128)S(1)}, f32[2,2,16]{2,1,0:T(2,128)S(1)}, u32[]{:S(2)}, u32[]{:S(2)}) collective-permute-start(f32[2,2,16]{2,1,0:T(2,128)S(1)} %get-tuple-element.18), channel_id=1, source_target_pairs={{0,2},{1,3},{2,0},{3,1},{4,6},{5,7},{6,4},{7,5},{8,10},{9,11},{10,... | collective-permute-start | bytes 776 | tf_op jit(solution)/shard_map/ppermute | solution.py:406
  66.7 0.0 collective-permute-start.6
  66.7 0.0 collective-permute-done.4.refs_1_
  66.7 2.2 %collective-permute-done.5.refs_2_ = f32[2,2,16]{2,1,0:T(2,128)S(1)} collective-permute-done((f32[2,2,16]{2,1,0:T(2,128)S(1)}, f32[2,2,16]{2,1,0:T(2,128)S(1)}, u32[]{:S(2)}, u32[]{:S(2)}) %collective-permute-start.5) | collective-permute-done | bytes 288 | tf_op jit(solution)/shard_map/ppermute | solution.py:406
  68.9 0.8 %collective-permute-done.6.refs_3_ = f32[2,2,16]{2,1,0:T(2,128)S(1)} collective-permute-done((f32[2,2,16]{2,1,0:T(2,128)S(1)}, f32[2,2,16]{2,1,0:T(2,128)S(1)}, u32[]{:S(2)}, u32[]{:S(2)}) %collective-permute-start.6) | collective-permute-done | bytes 288 | tf_op jit(solution)/shard_map/ppermute | solution.py:406
  69.7 1.9 %all-to-all-done.1.stats_ref = f32[8,1,16,128]{3,2,1,0:T(8,128)S(1)} async-done(((f32[8,1,16,128]{3,2,1,0:T(8,128)}), f32[8,1,16,128]{3,2,1,0:T(8,128)S(1)}, u32[]{:S(2)}, u32[]{:S(2)}) %all-to-all-start.1) | async-done | bytes 65568 | tf_op jit(solution)/shard_map/all_to_all | solution.py:421
  71.6 0.8 %finish.1 = (f32[2,4,8]{2,1,0:T(4,128)}, f32[2,2,16]{2,1,0:T(2,128)}) custom-call(f32[8,1,16,128]{3,2,1,0:T(8,128)S(1)} %all-to-all-done.1.stats_ref, f32[2,2,16]{2,1,0:T(2,128)S(1)} %get-tuple-element.16.gate_ref.refs_0_, f32[2,2,16]{2,1,0:T(2,128)S(1)} %collective-permute-done.4.refs_1_, f32[2,2,16]{2,1,0:T(2,128)S(1)} %collective-permute-done.5.refs_2_, ...), custom_call_target="tpu_custom_call" | custom-call | tf_op jit(solution)/shard_map/finish/pallas_call | solution.py:384
  (1 shorter events, 0.0 us)
Async XLA Ops:
  17.5 24.7 %collective-permute-start = (bf16[8,64,256]{2,1,0:T(8,128)(2,1)S(1)}, bf16[8,64,256]{2,1,0:T(8,128)(2,1)S(1)}, u32[]{:S(2)}, u32[]{:S(2)}) collective-permute-start(bf16[8,64,256]{2,1,0:T(8,128)(2,1)S(1)} %all_to_all.10.q_ref), channel_id=1, source_target_pairs={{0,1},{1,0},{2,3},{3,2},{4,5},{5,4},{6,7},{7,6},{8,9},{9,8},{10,11... | collective-permute-start | bytes 786440 | tf_op jit(solution)/shard_map/ppermute | solution.py:406
  17.5 4.7 %collective-permute-start.1 = (f32[8,128]{1,0:T(8,128)S(1)}, f32[8,128]{1,0:T(8,128)S(1)}, u32[]{:S(2)}, u32[]{:S(2)}) collective-permute-start(f32[8,128]{1,0:T(8,128)S(1)} %get-tuple-element.15.refs_0_), channel_id=1, source_target_pairs={{0,1},{1,0},{2,3},{3,2},{4,5},{5,4},{6,7},{7,6},{8,9},{9,8},{10,11... | collective-permute-start | bytes 12296 | tf_op jit(solution)/shard_map/ppermute | solution.py:406
  18.0 4.2 %collective-permute-start.2 = (f32[8,128]{1,0:T(8,128)S(1)}, f32[8,128]{1,0:T(8,128)S(1)}, u32[]{:S(2)}, u32[]{:S(2)}) collective-permute-start(f32[8,128]{1,0:T(8,128)S(1)} %get-tuple-element.15.refs_0_), channel_id=1, source_target_pairs={{0,2},{1,3},{2,0},{3,1},{4,6},{5,7},{6,4},{7,5},{8,10},{9,11},{10,... | collective-permute-start | bytes 12296 | tf_op jit(solution)/shard_map/ppermute | solution.py:406
  19.5 3.0 %collective-permute-start.3 = (f32[8,128]{1,0:T(8,128)S(1)}, f32[8,128]{1,0:T(8,128)S(1)}, u32[]{:S(2)}, u32[]{:S(2)}) collective-permute-start(f32[8,128]{1,0:T(8,128)S(1)} %get-tuple-element.15.refs_0_), channel_id=1, source_target_pairs={{0,3},{1,2},{2,1},{3,0},{4,7},{5,6},{6,5},{7,4},{8,11},{9,10},{10,... | collective-permute-start | bytes 12296 | tf_op jit(solution)/shard_map/ppermute | solution.py:406
  22.2 1.6 %copy-start = (bf16[4,1020,256]{2,0,1:T(4,128)(2,1)S(1)}, bf16[4,1020,256]{2,0,1:T(4,128)(2,1)}, u32[]{:S(2)}) copy-start(bf16[4,1020,256]{2,0,1:T(4,128)(2,1)} %param.8) | copy-start | bytes 6266884
  45.0 26.6 %all-to-all-start.1 = ((f32[8,1,16,128]{3,2,1,0:T(8,128)}), f32[8,1,16,128]{3,2,1,0:T(8,128)S(1)}, u32[]{:S(2)}, u32[]{:S(2)}) async-start(f32[8,1,16,128]{3,2,1,0:T(8,128)} %shard_map.87), calls=%async_computation.1 | async-start | bytes 131072 | tf_op jit(solution)/shard_map/all_to_all | solution.py:421
  64.6 2.1 %collective-permute-start.4 = (f32[2,2,16]{2,1,0:T(2,128)S(1)}, f32[2,2,16]{2,1,0:T(2,128)S(1)}, u32[]{:S(2)}, u32[]{:S(2)}) collective-permute-start(f32[2,2,16]{2,1,0:T(2,128)S(1)} %get-tuple-element.17), channel_id=1, source_target_pairs={{0,1},{1,0},{2,3},{3,2},{4,5},{5,4},{6,7},{7,6},{8,9},{9,8},{10,11... | collective-permute-start | bytes 776 | tf_op jit(solution)/shard_map/ppermute | solution.py:406
  65.3 3.6 %collective-permute-start.5 = (f32[2,2,16]{2,1,0:T(2,128)S(1)}, f32[2,2,16]{2,1,0:T(2,128)S(1)}, u32[]{:S(2)}, u32[]{:S(2)}) collective-permute-start(f32[2,2,16]{2,1,0:T(2,128)S(1)} %get-tuple-element.18), channel_id=1, source_target_pairs={{0,2},{1,3},{2,0},{3,1},{4,6},{5,7},{6,4},{7,5},{8,10},{9,11},{10,... | collective-permute-start | bytes 776 | tf_op jit(solution)/shard_map/ppermute | solution.py:406
  66.7 3.0 %collective-permute-start.6 = (f32[2,2,16]{2,1,0:T(2,128)S(1)}, f32[2,2,16]{2,1,0:T(2,128)S(1)}, u32[]{:S(2)}, u32[]{:S(2)}) collective-permute-start(f32[2,2,16]{2,1,0:T(2,128)S(1)} %get-tuple-element.19), channel_id=1, source_target_pairs={{0,3},{1,2},{2,1},{3,0},{4,7},{5,6},{6,5},{7,4},{8,11},{9,10},{10,... | collective-permute-start | bytes 776 | tf_op jit(solution)/shard_map/ppermute | solution.py:406

commit v4 on v3

--- a/solution.py
+++ b/solution.py
@@ -29,25 +29,30 @@
 
 
 def prepare_kernel(halves_ref, query_ref, pos_ref, mine_ref, pack_ref, half, query, pos, sems):
+    blocks = mine_ref.shape[0]
     core = lax.rem(lax.axis_index("frames"), 2)
-    copies = [
+    reads = [
         pltpu.make_async_copy(src, dst, sems.at[k])
         for k, (src, dst) in enumerate(
             ((halves_ref.at[core], half), (query_ref, query), (pos_ref, pos))
         )
     ]
-    for copy in copies:
+    writes = [pltpu.make_async_copy(half, mine_ref.at[k], sems.at[3 + k]) for k in range(blocks)]
+    for copy in reads:
         copy.start()
-    for copy in copies:
+    reads[0].wait()
+    for copy in writes:
+        copy.start()
+    for copy in reads[1:]:
         copy.wait()
-    for k in range(mine_ref.shape[0]):
-        mine_ref[k] = half[...]
     tracks = query.shape[0]
     window = pos.shape[2]
     pack_ref[...] = jnp.zeros(pack_ref.shape, jnp.float32)
     pack_ref[0:tracks, :] = query[...].astype(jnp.float32)
     for k in range(2):
         pack_ref[(k + 1) * tracks : (k + 2) * tracks, 0:window] = pos[k].astype(jnp.float32)
+    for copy in writes:
+        copy.wait()
 
 
 def prepare(blocks, halves, fine_query, places):
@@ -59,12 +64,12 @@
             jax.ShapeDtypeStruct((8, fine_query.shape[1]), jnp.float32),
         ],
         in_specs=[HBM] * 3,
-        out_specs=[VMEM] * 2,
+        out_specs=[HBM, VMEM],
         scratch_shapes=[
             pltpu.VMEM((rows, channels), halves.dtype),
             pltpu.VMEM(fine_query.shape, fine_query.dtype),
             pltpu.VMEM(places.shape, places.dtype),
-            pltpu.SemaphoreType.DMA((3,)),
+            pltpu.SemaphoreType.DMA((3 + blocks,)),
         ],
         compiler_params=SMALL,
         name="prepare",

time: 73 us -> 73.4 us (level)
  no operation moved by 1% of the time
where the time goes in v4:
time: 73.4 us; the launch traced here: 72.8 us
  Pallas kernels  26.8 us (37%)
  starting transfers between devices  23.7 us (32%)
  blocking collectives  16 us (22%)
  waiting for transfers between devices  5.2 us (7%)
    pallas_call x2, Pallas kernels, coarse_half(): pl.pallas_call(functools.partial(coarse_kernel, half), out_shape=jax.Shap...  21.2 us
    all_to_all x1, starting transfers between devices, body(): lax.all_to_all(stats, 'blk', split_axis=0, concat_axis=0, tiled=True)  19.6 us
    all_to_all x1, blocking collectives, body(): first = lax.all_to_all(mine, 'blk', split_axis=0, concat_axis=0, tiled=True)  16 us
    ppermute x7, starting transfers between devices, swap(): return lax.ppermute(x, 'frames', [(i, i ^ j) for i in range(owners)])  4.11 us
    ppermute x7, waiting for transfers between devices, swap(): return lax.ppermute(x, 'frames', [(i, i ^ j) for i in range(owners)])  3.27 us
    pallas_call x1, Pallas kernels, fetch(): pl.pallas_call(functools.partial(fetch_kernel, pieces, own), out_shape=[j...  2.69 us
    all_to_all x1, waiting for transfers between devices, body(): lax.all_to_all(stats, 'blk', split_axis=0, concat_axis=0, tiled=True)  1.93 us
  transfers between devices with their start and end apart: 8, of which 4 were waited for; matrix products, arithmetic and copies ran while one was open for 0% of the time, Pallas kernels for 30%

profile of v4, /device:TPU:0, one launch (start us, length us, event | category | flops | bytes accessed | tf_op | source)
XLA Modules:
  0.0 72.8 jit_solution(2047179993077336360)
XLA Ops:
  0.6 1.2 %prepare.1 = (bf16[8,64,256]{2,1,0:T(8,128)(2,1)S(1)}, f32[8,128]{1,0:T(8,128)S(1)}) custom-call(bf16[2,64,256]{2,1,0:T(8,128)(2,1)} %bitcast.6, bf16[2,128]{1,0:T(2,128)(2,1)} %query_ref.1, s32[2,2,16]{2,1,0:T(2,128)} %bitcast.7), custom_call_target="tpu_custom_call" | custom-call | tf_op jit(solution)/shard_map/prepare/pallas_call | solution.py:60
  1.8 16.0 %all_to_all.10.q_ref = bf16[8,64,256]{2,1,0:T(8,128)(2,1)S(1)} all-to-all(bf16[8,64,256]{2,1,0:T(8,128)(2,1)S(1)} %get-tuple-element.12), channel_id=1, replica_groups=mesh['blk'=8,'frames'=4] {'blk'}, dimensions={0} | all-to-all | bytes 524288 | tf_op jit(solution)/shard_map/all_to_all | solution.py:415
  17.8 0.0 collective-permute-start
  17.9 0.5 collective-permute-start.1
  18.4 1.5 %collective-permute-start.2 = (f32[8,128]{1,0:T(8,128)S(1)}, f32[8,128]{1,0:T(8,128)S(1)}, u32[]{:S(2)}, u32[]{:S(2)}) collective-permute-start(f32[8,128]{1,0:T(8,128)S(1)} %get-tuple-element.15.refs_0_), channel_id=1, source_target_pairs={{0,2},{1,3},{2,0},{3,1},{4,6},{5,7},{6,4},{7,5},{8,10},{9,11},{10,... | collective-permute-start | bytes 12296 | tf_op jit(solution)/shard_map/ppermute | solution.py:411
  19.9 0.0 collective-permute-start.3
  19.9 2.7 %fetch.1 = (bf16[4,4,8,64,128]{4,3,2,1,0:T(8,128)(2,1)S(1)}, f32[32,8]{1,0:T(8,128)S(1)}) custom-call(s32[4,1,4,8]{3,2,1,0:T(4,128)} %list_ref.1, s32[4,1,4,8]{3,2,1,0:T(4,128)} %list_ref.1, s32[4,1,4,8]{3,2,1,0:T(4,128)} %valid_ref.1, bf16[4,64,64,128]{3,2,1,0:T(8,128)(2,1)} %tiles_ref.1), custom_call_target="tpu_custom_call" | custom-call | tf_op jit(solution)/shard_map/fetch/pallas_call | solution.py:113
  22.6 0.0 copy-start
  22.6 0.0 collective-permute-done.1.refs_1_
  22.6 0.3 collective-permute-done.3.refs_3_
  22.9 0.9 %fine_part.1 = (f32[2,2,16]{2,1,0:T(2,128)S(1)}, f32[2,2,16]{2,1,0:T(2,128)S(1)}, f32[2,2,16]{2,1,0:T(2,128)S(1)}, f32[2,2,16]{2,1,0:T(2,128)S(1)}) custom-call(f32[32,8]{1,0:T(8,128)S(1)} %get-tuple-element.13.codes_ref, bf16[4,4,8,64,128]{4,3,2,1,0:T(8,128)(2,1)S(1)} %get-tuple-element.14.tiles_ref, f32[8,128]{1,0:T(8,128)S(1)} %get-tuple-element.15.refs_0_, ...), custom_call_target="tpu_custom_call" | custom-call | tf_op jit(solution)/shard_map/fine_part/pallas_call | solution.py:197
  23.7 0.4 copy-done
  24.1 18.4 %shard_map.86.rest_0_ = f32[8,1,16,128]{3,2,1,0:T(8,128)S(1)} custom-call(bf16[8,64,256]{2,1,0:T(8,128)(2,1)S(1)} %all_to_all.10.q_ref, bf16[1020,4,256]{2,1,0:T(4,128)(2,1)S(1)} %bitcast.4, f32[2,2,16]{2,1,0:T(2,128)S(1)} %get-tuple-element.16.gate_ref.refs_0_), custom_call_target="tpu_custom_call" | custom-call | tf_op jit(solution)/shard_map/pallas_call | solution.py:331
  42.5 0.0 collective-permute-done.q_ref
  42.5 2.9 %shard_map.87 = f32[8,1,16,128]{3,2,1,0:T(8,128)} custom-call(bf16[8,64,256]{2,1,0:T(8,128)(2,1)S(1)} %collective-permute-done.q_ref, bf16[1020,4,256]{2,1,0:T(4,128)(2,1)S(1)} %bitcast.5, f32[2,2,16]{2,1,0:T(2,128)S(1)} %get-tuple-element.16.gate_ref.refs_0_, f32[8,1,16,128]{3,2,1,0:T(8,128)S(1)} %shard_map.86.rest_0_), custom_call_target="tpu_custom_call" | custom-call | tf_op jit(solution)/shard_map/pallas_call | solution.py:331
  45.4 19.6 %all-to-all-start.1 = ((f32[8,1,16,128]{3,2,1,0:T(8,128)}), f32[8,1,16,128]{3,2,1,0:T(8,128)S(1)}, u32[]{:S(2)}, u32[]{:S(2)}) async-start(f32[8,1,16,128]{3,2,1,0:T(8,128)} %shard_map.87), calls=%async_computation.1 | async-start | bytes 131072 | tf_op jit(solution)/shard_map/all_to_all | solution.py:426
  65.0 0.7 collective-permute-start.4
  65.7 1.4 %collective-permute-start.5 = (f32[2,2,16]{2,1,0:T(2,128)S(1)}, f32[2,2,16]{2,1,0:T(2,128)S(1)}, u32[]{:S(2)}, u32[]{:S(2)}) collective-permute-start(f32[2,2,16]{2,1,0:T(2,128)S(1)} %get-tuple-element.18), channel_id=1, source_target_pairs={{0,2},{1,3},{2,0},{3,1},{4,6},{5,7},{6,4},{7,5},{8,10},{9,11},{10,... | collective-permute-start | bytes 776 | tf_op jit(solution)/shard_map/ppermute | solution.py:411
  67.1 0.0 collective-permute-start.6
  67.1 0.0 collective-permute-done.4.refs_1_
  67.1 2.2 %collective-permute-done.5.refs_2_ = f32[2,2,16]{2,1,0:T(2,128)S(1)} collective-permute-done((f32[2,2,16]{2,1,0:T(2,128)S(1)}, f32[2,2,16]{2,1,0:T(2,128)S(1)}, u32[]{:S(2)}, u32[]{:S(2)}) %collective-permute-start.5) | collective-permute-done | bytes 288 | tf_op jit(solution)/shard_map/ppermute | solution.py:411
  69.3 0.8 %collective-permute-done.6.refs_3_ = f32[2,2,16]{2,1,0:T(2,128)S(1)} collective-permute-done((f32[2,2,16]{2,1,0:T(2,128)S(1)}, f32[2,2,16]{2,1,0:T(2,128)S(1)}, u32[]{:S(2)}, u32[]{:S(2)}) %collective-permute-start.6) | collective-permute-done | bytes 288 | tf_op jit(solution)/shard_map/ppermute | solution.py:411
  70.1 1.9 %all-to-all-done.1.stats_ref = f32[8,1,16,128]{3,2,1,0:T(8,128)S(1)} async-done(((f32[8,1,16,128]{3,2,1,0:T(8,128)}), f32[8,1,16,128]{3,2,1,0:T(8,128)S(1)}, u32[]{:S(2)}, u32[]{:S(2)}) %all-to-all-start.1) | async-done | bytes 65568 | tf_op jit(solution)/shard_map/all_to_all | solution.py:426
  72.0 0.8 %finish.1 = (f32[2,4,8]{2,1,0:T(4,128)}, f32[2,2,16]{2,1,0:T(2,128)}) custom-call(f32[8,1,16,128]{3,2,1,0:T(8,128)S(1)} %all-to-all-done.1.stats_ref, f32[2,2,16]{2,1,0:T(2,128)S(1)} %get-tuple-element.16.gate_ref.refs_0_, f32[2,2,16]{2,1,0:T(2,128)S(1)} %collective-permute-done.4.refs_1_, f32[2,2,16]{2,1,0:T(2,128)S(1)} %collective-permute-done.5.refs_2_, ...), custom_call_target="tpu_custom_call" | custom-call | tf_op jit(solution)/shard_map/finish/pallas_call | solution.py:389
  (1 shorter events, 0.0 us)
Async XLA Ops:
  17.8 24.7 %collective-permute-start = (bf16[8,64,256]{2,1,0:T(8,128)(2,1)S(1)}, bf16[8,64,256]{2,1,0:T(8,128)(2,1)S(1)}, u32[]{:S(2)}, u32[]{:S(2)}) collective-permute-start(bf16[8,64,256]{2,1,0:T(8,128)(2,1)S(1)} %all_to_all.10.q_ref), channel_id=1, source_target_pairs={{0,1},{1,0},{2,3},{3,2},{4,5},{5,4},{6,7},{7,6},{8,9},{9,8},{10,11... | collective-permute-start | bytes 786440 | tf_op jit(solution)/shard_map/ppermute | solution.py:411
  17.9 4.7 %collective-permute-start.1 = (f32[8,128]{1,0:T(8,128)S(1)}, f32[8,128]{1,0:T(8,128)S(1)}, u32[]{:S(2)}, u32[]{:S(2)}) collective-permute-start(f32[8,128]{1,0:T(8,128)S(1)} %get-tuple-element.15.refs_0_), channel_id=1, source_target_pairs={{0,1},{1,0},{2,3},{3,2},{4,5},{5,4},{6,7},{7,6},{8,9},{9,8},{10,11... | collective-permute-start | bytes 12296 | tf_op jit(solution)/shard_map/ppermute | solution.py:411
  18.4 4.2 %collective-permute-start.2 = (f32[8,128]{1,0:T(8,128)S(1)}, f32[8,128]{1,0:T(8,128)S(1)}, u32[]{:S(2)}, u32[]{:S(2)}) collective-permute-start(f32[8,128]{1,0:T(8,128)S(1)} %get-tuple-element.15.refs_0_), channel_id=1, source_target_pairs={{0,2},{1,3},{2,0},{3,1},{4,6},{5,7},{6,4},{7,5},{8,10},{9,11},{10,... | collective-permute-start | bytes 12296 | tf_op jit(solution)/shard_map/ppermute | solution.py:411
  19.9 3.0 %collective-permute-start.3 = (f32[8,128]{1,0:T(8,128)S(1)}, f32[8,128]{1,0:T(8,128)S(1)}, u32[]{:S(2)}, u32[]{:S(2)}) collective-permute-start(f32[8,128]{1,0:T(8,128)S(1)} %get-tuple-element.15.refs_0_), channel_id=1, source_target_pairs={{0,3},{1,2},{2,1},{3,0},{4,7},{5,6},{6,5},{7,4},{8,11},{9,10},{10,... | collective-permute-start | bytes 12296 | tf_op jit(solution)/shard_map/ppermute | solution.py:411
  22.6 1.6 %copy-start = (bf16[4,1020,256]{2,0,1:T(4,128)(2,1)S(1)}, bf16[4,1020,256]{2,0,1:T(4,128)(2,1)}, u32[]{:S(2)}) copy-start(bf16[4,1020,256]{2,0,1:T(4,128)(2,1)} %param.8) | copy-start | bytes 6266884
  45.4 26.6 %all-to-all-start.1 = ((f32[8,1,16,128]{3,2,1,0:T(8,128)}), f32[8,1,16,128]{3,2,1,0:T(8,128)S(1)}, u32[]{:S(2)}, u32[]{:S(2)}) async-start(f32[8,1,16,128]{3,2,1,0:T(8,128)} %shard_map.87), calls=%async_computation.1 | async-start | bytes 131072 | tf_op jit(solution)/shard_map/all_to_all | solution.py:426
  65.0 2.1 %collective-permute-start.4 = (f32[2,2,16]{2,1,0:T(2,128)S(1)}, f32[2,2,16]{2,1,0:T(2,128)S(1)}, u32[]{:S(2)}, u32[]{:S(2)}) collective-permute-start(f32[2,2,16]{2,1,0:T(2,128)S(1)} %get-tuple-element.17), channel_id=1, source_target_pairs={{0,1},{1,0},{2,3},{3,2},{4,5},{5,4},{6,7},{7,6},{8,9},{9,8},{10,11... | collective-permute-start | bytes 776 | tf_op jit(solution)/shard_map/ppermute | solution.py:411
  65.7 3.6 %collective-permute-start.5 = (f32[2,2,16]{2,1,0:T(2,128)S(1)}, f32[2,2,16]{2,1,0:T(2,128)S(1)}, u32[]{:S(2)}, u32[]{:S(2)}) collective-permute-start(f32[2,2,16]{2,1,0:T(2,128)S(1)} %get-tuple-element.18), channel_id=1, source_target_pairs={{0,2},{1,3},{2,0},{3,1},{4,6},{5,7},{6,4},{7,5},{8,10},{9,11},{10,... | collective-permute-start | bytes 776 | tf_op jit(solution)/shard_map/ppermute | solution.py:411
  67.1 3.0 %collective-permute-start.6 = (f32[2,2,16]{2,1,0:T(2,128)S(1)}, f32[2,2,16]{2,1,0:T(2,128)S(1)}, u32[]{:S(2)}, u32[]{:S(2)}) collective-permute-start(f32[2,2,16]{2,1,0:T(2,128)S(1)} %get-tuple-element.19), channel_id=1, source_target_pairs={{0,3},{1,2},{2,1},{3,0},{4,7},{5,6},{6,5},{7,4},{8,11},{9,10},{10,... | collective-permute-start | bytes 776 | tf_op jit(solution)/shard_map/ppermute | solution.py:411

commit v5 on v4

--- a/solution.py
+++ b/solution.py
@@ -410,9 +410,12 @@
     def swap(x, j):
         return lax.ppermute(x, "frames", [(i, i ^ j) for i in range(owners)])
 
+    ranks = [sorted(range(blocks), key=lambda b: (abs(b - blocks // 2), b))]
     halves = coarse_query.reshape(2, tracks * heads // 2, channels)
     mine, payload = prepare(blocks, halves, fine_query, jnp.transpose(track_pos, (0, 2, 1)))
-    first = lax.all_to_all(mine, "blk", split_axis=0, concat_axis=0, tiled=True)
+    first = lax.all_to_all(
+        mine, "blk", split_axis=0, concat_axis=0, tiled=True, axis_index_groups=ranks
+    )
     payloads = [payload] + [swap(payload, j) for j in range(1, owners)]
     tiles, codes = fetch(tile_list, tile_valid, fine_tiles, owners, own)
     fine = fine_part(codes, tiles, own, window, region, payloads)
@@ -423,7 +426,9 @@
     second = swap(first, 1)
     stats = coarse_half(first, cells, gate)
     stats = coarse_half(second, cells, gate, stats)
-    stats = lax.all_to_all(stats, "blk", split_axis=0, concat_axis=0, tiled=True)
+    stats = lax.all_to_all(
+        stats, "blk", split_axis=0, concat_axis=0, tiled=True, axis_index_groups=ranks
+    )
     coarse_pos, fine_offset = finish(stats, fine, heads, channels)
     return coarse_pos, jnp.transpose(fine_offset, (0, 2, 1))
 

time: 73.4 us -> 70.4 us (0.959)
  waiting for transfers between devices: 5.2 us -> 3.17 us
  blocking collectives: 16 us -> 14.8 us
    all_to_all x1, waiting for transfers between devices: 1.93 us -> 0.01 us  [body(): lax.all_to_all(stats, 'blk', split_axis=0, concat_axis=0, tiled=True, axi...]
    all_to_all x1, blocking collectives: 16 us -> 14.8 us  [body(): lax.all_to_all(mine, 'blk', split_axis=0, concat_axis=0, tiled=True, axis...]
  transfers between devices with their start and end apart: 8 -> 8, of which waited for: 4 -> 3; matrix products, arithmetic and copies ran while one was open for 0% -> 0% of each run, Pallas kernels for 30% -> 31%
where the time goes in v5:
time: 70.4 us; the launch traced here: 69.9 us
  Pallas kernels  26.8 us (38%)
  starting transfers between devices  24 us (34%)
  blocking collectives  14.8 us (21%)
  waiting for transfers between devices  3.17 us (5%)
    pallas_call x2, Pallas kernels, coarse_half(): pl.pallas_call(functools.partial(coarse_kernel, half), out_shape=jax.Shap...  21.2 us
    all_to_all x1, starting transfers between devices, body(): lax.all_to_all(stats, 'blk', split_axis=0, concat_axis=0, tiled=True, axi...  20.2 us
    all_to_all x1, blocking collectives, body(): lax.all_to_all(mine, 'blk', split_axis=0, concat_axis=0, tiled=True, axis...  14.8 us
    ppermute x7, starting transfers between devices, swap(): return lax.ppermute(x, 'frames', [(i, i ^ j) for i in range(owners)])  3.86 us
    ppermute x7, waiting for transfers between devices, swap(): return lax.ppermute(x, 'frames', [(i, i ^ j) for i in range(owners)])  3.17 us
    pallas_call x1, Pallas kernels, fetch(): pl.pallas_call(functools.partial(fetch_kernel, pieces, own), out_shape=[j...  2.69 us
  transfers between devices with their start and end apart: 8, of which 3 were waited for; matrix products, arithmetic and copies ran while one was open for 0% of the time, Pallas kernels for 31%

profile of v5, /device:TPU:0, one launch (start us, length us, event | category | flops | bytes accessed | tf_op | source)
XLA Modules:
  0.0 69.9 jit_solution(5453867211705991827)
XLA Ops:
  0.6 1.2 %prepare.1 = (bf16[8,64,256]{2,1,0:T(8,128)(2,1)S(1)}, f32[8,128]{1,0:T(8,128)S(1)}) custom-call(bf16[2,64,256]{2,1,0:T(8,128)(2,1)} %bitcast.6, bf16[2,128]{1,0:T(2,128)(2,1)} %query_ref.1, s32[2,2,16]{2,1,0:T(2,128)} %bitcast.7), custom_call_target="tpu_custom_call" | custom-call | tf_op jit(solution)/shard_map/prepare/pallas_call | solution.py:60
  1.8 14.8 %all_to_all.10.q_ref = bf16[8,64,256]{2,1,0:T(8,128)(2,1)S(1)} all-to-all(bf16[8,64,256]{2,1,0:T(8,128)(2,1)S(1)} %get-tuple-element.12), channel_id=1, replica_groups={{16,12,20,8,24,4,28,0},{17,13,21,9,25,5,29,1},{18,14,22,10,26,6,30,2},{..., dimensions={0} | all-to-all | bytes 524288 | tf_op jit(solution)/shard_map/all_to_all | solution.py:416
  16.6 0.0 collective-permute-start
  16.6 0.5 collective-permute-start.1
  17.1 1.5 %collective-permute-start.2 = (f32[8,128]{1,0:T(8,128)S(1)}, f32[8,128]{1,0:T(8,128)S(1)}, u32[]{:S(2)}, u32[]{:S(2)}) collective-permute-start(f32[8,128]{1,0:T(8,128)S(1)} %get-tuple-element.15.refs_0_), channel_id=1, source_target_pairs={{0,2},{1,3},{2,0},{3,1},{4,6},{5,7},{6,4},{7,5},{8,10},{9,11},{10,... | collective-permute-start | bytes 12296 | tf_op jit(solution)/shard_map/ppermute | solution.py:411
  18.6 0.0 collective-permute-start.3
  18.6 2.7 %fetch.1 = (bf16[4,4,8,64,128]{4,3,2,1,0:T(8,128)(2,1)S(1)}, f32[32,8]{1,0:T(8,128)S(1)}) custom-call(s32[4,1,4,8]{3,2,1,0:T(4,128)} %list_ref.1, s32[4,1,4,8]{3,2,1,0:T(4,128)} %list_ref.1, s32[4,1,4,8]{3,2,1,0:T(4,128)} %valid_ref.1, bf16[4,64,64,128]{3,2,1,0:T(8,128)(2,1)} %tiles_ref.1), custom_call_target="tpu_custom_call" | custom-call | tf_op jit(solution)/shard_map/fetch/pallas_call | solution.py:113
  21.3 0.0 copy-start
  21.3 0.0 collective-permute-done.1.refs_1_
  21.3 0.0 collective-permute-done.2.refs_2_
  21.3 0.3 collective-permute-done.3.refs_3_
  21.6 0.9 %fine_part.1 = (f32[2,2,16]{2,1,0:T(2,128)S(1)}, f32[2,2,16]{2,1,0:T(2,128)S(1)}, f32[2,2,16]{2,1,0:T(2,128)S(1)}, f32[2,2,16]{2,1,0:T(2,128)S(1)}) custom-call(f32[32,8]{1,0:T(8,128)S(1)} %get-tuple-element.13.codes_ref, bf16[4,4,8,64,128]{4,3,2,1,0:T(8,128)(2,1)S(1)} %get-tuple-element.14.tiles_ref, f32[8,128]{1,0:T(8,128)S(1)} %get-tuple-element.15.refs_0_, ...), custom_call_target="tpu_custom_call" | custom-call | tf_op jit(solution)/shard_map/fine_part/pallas_call | solution.py:197
  22.5 0.4 copy-done
  22.9 18.4 %shard_map.86.rest_0_ = f32[8,1,16,128]{3,2,1,0:T(8,128)S(1)} custom-call(bf16[8,64,256]{2,1,0:T(8,128)(2,1)S(1)} %all_to_all.10.q_ref, bf16[1020,4,256]{2,1,0:T(4,128)(2,1)S(1)} %bitcast.4, f32[2,2,16]{2,1,0:T(2,128)S(1)} %get-tuple-element.16.gate_ref.refs_0_), custom_call_target="tpu_custom_call" | custom-call | tf_op jit(solution)/shard_map/pallas_call | solution.py:331
  41.3 0.0 collective-permute-done.q_ref
  41.3 2.9 %shard_map.87 = f32[8,1,16,128]{3,2,1,0:T(8,128)} custom-call(bf16[8,64,256]{2,1,0:T(8,128)(2,1)S(1)} %collective-permute-done.q_ref, bf16[1020,4,256]{2,1,0:T(4,128)(2,1)S(1)} %bitcast.5, f32[2,2,16]{2,1,0:T(2,128)S(1)} %get-tuple-element.16.gate_ref.refs_0_, f32[8,1,16,128]{3,2,1,0:T(8,128)S(1)} %shard_map.86.rest_0_), custom_call_target="tpu_custom_call" | custom-call | tf_op jit(solution)/shard_map/pallas_call | solution.py:331
  44.1 20.2 %all-to-all-start.1 = ((f32[8,1,16,128]{3,2,1,0:T(8,128)}), f32[8,1,16,128]{3,2,1,0:T(8,128)S(1)}, u32[]{:S(2)}, u32[]{:S(2)}) async-start(f32[8,1,16,128]{3,2,1,0:T(8,128)} %shard_map.87), calls=%async_computation.1 | async-start | bytes 131072 | tf_op jit(solution)/shard_map/all_to_all | solution.py:429
  64.3 0.3 collective-permute-start.4
  64.6 1.4 %collective-permute-start.5 = (f32[2,2,16]{2,1,0:T(2,128)S(1)}, f32[2,2,16]{2,1,0:T(2,128)S(1)}, u32[]{:S(2)}, u32[]{:S(2)}) collective-permute-start(f32[2,2,16]{2,1,0:T(2,128)S(1)} %get-tuple-element.18), channel_id=1, source_target_pairs={{0,2},{1,3},{2,0},{3,1},{4,6},{5,7},{6,4},{7,5},{8,10},{9,11},{10,... | collective-permute-start | bytes 776 | tf_op jit(solution)/shard_map/ppermute | solution.py:411
  66.0 0.1 collective-permute-start.6
  66.2 0.0 collective-permute-done.4.refs_1_
  66.2 2.0 %collective-permute-done.5.refs_2_ = f32[2,2,16]{2,1,0:T(2,128)S(1)} collective-permute-done((f32[2,2,16]{2,1,0:T(2,128)S(1)}, f32[2,2,16]{2,1,0:T(2,128)S(1)}, u32[]{:S(2)}, u32[]{:S(2)}) %collective-permute-start.5) | collective-permute-done | bytes 288 | tf_op jit(solution)/shard_map/ppermute | solution.py:411
  68.2 0.8 %collective-permute-done.6.refs_3_ = f32[2,2,16]{2,1,0:T(2,128)S(1)} collective-permute-done((f32[2,2,16]{2,1,0:T(2,128)S(1)}, f32[2,2,16]{2,1,0:T(2,128)S(1)}, u32[]{:S(2)}, u32[]{:S(2)}) %collective-permute-start.6) | collective-permute-done | bytes 288 | tf_op jit(solution)/shard_map/ppermute | solution.py:411
  69.0 0.8 %finish.1 = (f32[2,4,8]{2,1,0:T(4,128)}, f32[2,2,16]{2,1,0:T(2,128)}) custom-call(f32[8,1,16,128]{3,2,1,0:T(8,128)S(1)} %all-to-all-done.1.stats_ref, f32[2,2,16]{2,1,0:T(2,128)S(1)} %get-tuple-element.16.gate_ref.refs_0_, f32[2,2,16]{2,1,0:T(2,128)S(1)} %collective-permute-done.4.refs_1_, f32[2,2,16]{2,1,0:T(2,128)S(1)} %collective-permute-done.5.refs_2_, ...), custom_call_target="tpu_custom_call" | custom-call | tf_op jit(solution)/shard_map/finish/pallas_call | solution.py:389
  (1 shorter events, 0.0 us)
Async XLA Ops:
  16.6 24.7 %collective-permute-start = (bf16[8,64,256]{2,1,0:T(8,128)(2,1)S(1)}, bf16[8,64,256]{2,1,0:T(8,128)(2,1)S(1)}, u32[]{:S(2)}, u32[]{:S(2)}) collective-permute-start(bf16[8,64,256]{2,1,0:T(8,128)(2,1)S(1)} %all_to_all.10.q_ref), channel_id=1, source_target_pairs={{0,1},{1,0},{2,3},{3,2},{4,5},{5,4},{6,7},{7,6},{8,9},{9,8},{10,11... | collective-permute-start | bytes 786440 | tf_op jit(solution)/shard_map/ppermute | solution.py:411
  16.6 4.7 %collective-permute-start.1 = (f32[8,128]{1,0:T(8,128)S(1)}, f32[8,128]{1,0:T(8,128)S(1)}, u32[]{:S(2)}, u32[]{:S(2)}) collective-permute-start(f32[8,128]{1,0:T(8,128)S(1)} %get-tuple-element.15.refs_0_), channel_id=1, source_target_pairs={{0,1},{1,0},{2,3},{3,2},{4,5},{5,4},{6,7},{7,6},{8,9},{9,8},{10,11... | collective-permute-start | bytes 12296 | tf_op jit(solution)/shard_map/ppermute | solution.py:411
  17.1 4.2 %collective-permute-start.2 = (f32[8,128]{1,0:T(8,128)S(1)}, f32[8,128]{1,0:T(8,128)S(1)}, u32[]{:S(2)}, u32[]{:S(2)}) collective-permute-start(f32[8,128]{1,0:T(8,128)S(1)} %get-tuple-element.15.refs_0_), channel_id=1, source_target_pairs={{0,2},{1,3},{2,0},{3,1},{4,6},{5,7},{6,4},{7,5},{8,10},{9,11},{10,... | collective-permute-start | bytes 12296 | tf_op jit(solution)/shard_map/ppermute | solution.py:411
  18.6 3.0 %collective-permute-start.3 = (f32[8,128]{1,0:T(8,128)S(1)}, f32[8,128]{1,0:T(8,128)S(1)}, u32[]{:S(2)}, u32[]{:S(2)}) collective-permute-start(f32[8,128]{1,0:T(8,128)S(1)} %get-tuple-element.15.refs_0_), channel_id=1, source_target_pairs={{0,3},{1,2},{2,1},{3,0},{4,7},{5,6},{6,5},{7,4},{8,11},{9,10},{10,... | collective-permute-start | bytes 12296 | tf_op jit(solution)/shard_map/ppermute | solution.py:411
  21.3 1.6 %copy-start = (bf16[4,1020,256]{2,0,1:T(4,128)(2,1)S(1)}, bf16[4,1020,256]{2,0,1:T(4,128)(2,1)}, u32[]{:S(2)}) copy-start(bf16[4,1020,256]{2,0,1:T(4,128)(2,1)} %param.8) | copy-start | bytes 6266884
  44.1 24.9 %all-to-all-start.1 = ((f32[8,1,16,128]{3,2,1,0:T(8,128)}), f32[8,1,16,128]{3,2,1,0:T(8,128)S(1)}, u32[]{:S(2)}, u32[]{:S(2)}) async-start(f32[8,1,16,128]{3,2,1,0:T(8,128)} %shard_map.87), calls=%async_computation.1 | async-start | bytes 131072 | tf_op jit(solution)/shard_map/all_to_all | solution.py:429
  64.3 1.9 %collective-permute-start.4 = (f32[2,2,16]{2,1,0:T(2,128)S(1)}, f32[2,2,16]{2,1,0:T(2,128)S(1)}, u32[]{:S(2)}, u32[]{:S(2)}) collective-permute-start(f32[2,2,16]{2,1,0:T(2,128)S(1)} %get-tuple-element.17), channel_id=1, source_target_pairs={{0,1},{1,0},{2,3},{3,2},{4,5},{5,4},{6,7},{7,6},{8,9},{9,8},{10,11... | collective-permute-start | bytes 776 | tf_op jit(solution)/shard_map/ppermute | solution.py:411
  64.6 3.6 %collective-permute-start.5 = (f32[2,2,16]{2,1,0:T(2,128)S(1)}, f32[2,2,16]{2,1,0:T(2,128)S(1)}, u32[]{:S(2)}, u32[]{:S(2)}) collective-permute-start(f32[2,2,16]{2,1,0:T(2,128)S(1)} %get-tuple-element.18), channel_id=1, source_target_pairs={{0,2},{1,3},{2,0},{3,1},{4,6},{5,7},{6,4},{7,5},{8,10},{9,11},{10,... | collective-permute-start | bytes 776 | tf_op jit(solution)/shard_map/ppermute | solution.py:411
  66.0 3.0 %collective-permute-start.6 = (f32[2,2,16]{2,1,0:T(2,128)S(1)}, f32[2,2,16]{2,1,0:T(2,128)S(1)}, u32[]{:S(2)}, u32[]{:S(2)}) collective-permute-start(f32[2,2,16]{2,1,0:T(2,128)S(1)} %get-tuple-element.19), channel_id=1, source_target_pairs={{0,3},{1,2},{2,1},{3,0},{4,7},{5,6},{6,5},{7,4},{8,11},{9,10},{10,... | collective-permute-start | bytes 776 | tf_op jit(solution)/shard_map/ppermute | solution.py:411

commit v6 on v5

--- a/solution.py
+++ b/solution.py
@@ -28,16 +28,26 @@
     return pltpu.with_memory_space_constraint(x, pltpu.HBM)
 
 
-def prepare_kernel(halves_ref, query_ref, pos_ref, mine_ref, pack_ref, half, query, pos, sems):
+def prepare_kernel(
+    pieces, own, halves_ref, query_ref, pos_ref, list_ref, valid_ref,
+    mine_ref, pack_ref, ids_ref, codes_ref, half, query, pos, live, sems,
+):
     blocks = mine_ref.shape[0]
-    core = lax.rem(lax.axis_index("frames"), 2)
+    frames = ids_ref.shape[0]
+    me = lax.axis_index("frames")
     reads = [
         pltpu.make_async_copy(src, dst, sems.at[k])
         for k, (src, dst) in enumerate(
-            ((halves_ref.at[core], half), (query_ref, query), (pos_ref, pos))
+            (
+                (halves_ref.at[lax.rem(me, 2)], half),
+                (query_ref, query),
+                (pos_ref, pos),
+                (list_ref, ids_ref),
+                (valid_ref, live),
+            )
         )
     ]
-    writes = [pltpu.make_async_copy(half, mine_ref.at[k], sems.at[3 + k]) for k in range(blocks)]
+    writes = [pltpu.make_async_copy(half, mine_ref.at[k], sems.at[5 + k]) for k in range(blocks)]
     for copy in reads:
         copy.start()
     reads[0].wait()
@@ -45,97 +55,87 @@
         copy.start()
     for copy in reads[1:]:
         copy.wait()
-    tracks = query.shape[0]
     window = pos.shape[2]
     pack_ref[...] = jnp.zeros(pack_ref.shape, jnp.float32)
-    pack_ref[0:tracks, :] = query[...].astype(jnp.float32)
+    pack_ref[0:own, :] = query[...].astype(jnp.float32)
     for k in range(2):
-        pack_ref[(k + 1) * tracks : (k + 2) * tracks, 0:window] = pos[k].astype(jnp.float32)
+        pack_ref[(k + 1) * own : (k + 2) * own, 0:window] = pos[k].astype(jnp.float32)
+    for i in range(frames):
+        for j in range(pieces):
+            owner = pl.ds(lax.bitwise_xor(me, j), 1)
+            code = jnp.where(live[i, 0, owner, :] > 0, ids_ref[i, 0, owner, :], -1)
+            for k in range(own):
+                row = (i * pieces + j) * own + k
+                codes_ref[row : row + 1, :] = code.astype(jnp.float32)
     for copy in writes:
         copy.wait()
 
 
-def prepare(blocks, halves, fine_query, places):
+def prepare(blocks, pieces, halves, fine_query, places, tile_list, tile_valid):
     _, rows, channels = halves.shape
+    own = fine_query.shape[0]
+    frames, _, _, slots = tile_list.shape
+    arrays = (halves, fine_query, places, tile_list, tile_valid)
     return pl.pallas_call(
-        prepare_kernel,
+        functools.partial(prepare_kernel, pieces, own),
         out_shape=[
             jax.ShapeDtypeStruct((blocks, rows, channels), halves.dtype),
             jax.ShapeDtypeStruct((8, fine_query.shape[1]), jnp.float32),
+            jax.ShapeDtypeStruct(tile_list.shape, tile_list.dtype),
+            jax.ShapeDtypeStruct((frames * pieces * own, slots), jnp.float32),
         ],
-        in_specs=[HBM] * 3,
-        out_specs=[HBM, VMEM],
+        in_specs=[HBM] * 5,
+        out_specs=[HBM, VMEM, VMEM, VMEM],
         scratch_shapes=[
             pltpu.VMEM((rows, channels), halves.dtype),
             pltpu.VMEM(fine_query.shape, fine_query.dtype),
             pltpu.VMEM(places.shape, places.dtype),
-            pltpu.SemaphoreType.DMA((3 + blocks,)),
+            pltpu.VMEM(tile_valid.shape, tile_valid.dtype),
+            pltpu.SemaphoreType.DMA((5 + blocks,)),
         ],
         compiler_params=SMALL,
         name="prepare",
-    )(*(stay(x) for x in (halves, fine_query, places)))
-
-
-def fetch_kernel(pieces, own, ids_ref, list_ref, valid_ref, tiles_ref, out_ref, codes_ref, ids, live, sems):
+    )(*(stay(x) for x in arrays))
+
+
+def fetch_kernel(pieces, ids_ref, tiles_ref, out_ref, sems):
     frames, _, slots = out_ref.shape[:3]
     me = lax.axis_index("frames")
-    copies = [
-        pltpu.make_async_copy(list_ref, ids, sems.at[frames]),
-        pltpu.make_async_copy(valid_ref, live, sems.at[frames + 1]),
-    ]
-    for copy in copies:
-        copy.start()
     for i in range(frames):
-        for j in range(pieces):
+        for owner in range(pieces):
+            slot = out_ref.at[i, lax.bitwise_xor(me, owner)]
             for s in range(slots):
-                tile = ids_ref[i, 0, lax.bitwise_xor(me, j), s]
                 pltpu.make_async_copy(
-                    tiles_ref.at[i, tile], out_ref.at[i, j, s], sems.at[i]
+                    tiles_ref.at[i, ids_ref[i, 0, owner, s]], slot.at[s], sems.at[i]
                 ).start()
-    for copy in copies:
-        copy.wait()
-    for i in range(frames):
-        for j in range(pieces):
-            owner = lax.bitwise_xor(me, j)
-            code = jnp.where(
-                live[i, 0, pl.ds(owner, 1), :] > 0, ids[i, 0, pl.ds(owner, 1), :], -1
-            ).astype(jnp.float32)
-            for k in range(own):
-                row = (i * pieces + j) * own + k
-                codes_ref[row : row + 1, :] = code
     for i in range(frames):
         pltpu.make_async_copy(out_ref.at[i], out_ref.at[i], sems.at[i]).wait()
 
 
-def fetch(tile_list, tile_valid, fine_tiles, pieces, own):
+def fetch(ids, fine_tiles, pieces):
     frames, _, cells, channels = fine_tiles.shape
-    slots = tile_list.shape[3]
+    slots = ids.shape[3]
     return pl.pallas_call(
-        functools.partial(fetch_kernel, pieces, own),
-        out_shape=[
-            jax.ShapeDtypeStruct((frames, pieces, slots, cells, channels), fine_tiles.dtype),
-            jax.ShapeDtypeStruct((frames * pieces * own, slots), jnp.float32),
-        ],
-        in_specs=[SMEM, HBM, HBM, HBM],
-        out_specs=[VMEM] * 2,
-        scratch_shapes=[
-            pltpu.VMEM(tile_list.shape, tile_list.dtype),
-            pltpu.VMEM(tile_valid.shape, tile_valid.dtype),
-            pltpu.SemaphoreType.DMA((frames + 2,)),
-        ],
+        functools.partial(fetch_kernel, pieces),
+        out_shape=jax.ShapeDtypeStruct(
+            (frames, pieces, slots, cells, channels), fine_tiles.dtype
+        ),
+        in_specs=[SMEM, HBM],
+        out_specs=VMEM,
+        scratch_shapes=[pltpu.SemaphoreType.DMA((frames,))],
         compiler_params=SMALL,
         name="fetch",
-    )(tile_list, *(stay(x) for x in (tile_list, tile_valid, fine_tiles)))
+    )(ids, stay(fine_tiles))
 
 
 def fine_kernel(pieces, own, region, codes_ref, tiles_ref, *refs):
-    ins, outs = refs[:pieces], refs[pieces:]
+    ins, evens, odd_ref = refs[:pieces], refs[pieces:-1], refs[-1]
     frames, _, slots, cells, channels = tiles_ref.shape
     tracks = pieces * own
     wide = slots * cells
     base = lax.axis_index("blk") * region
     me = lax.axis_index("frames")
-    window = outs[0].shape[2]
+    window = odd_ref.shape[3]
     scale = 1.0 / math.sqrt(channels)
     query = jnp.concatenate([r[0:own, :] for r in ins], axis=0).astype(jnp.bfloat16)
     rows_in = jnp.concatenate([r[own : 2 * own, :] for r in ins], axis=0)
@@ -188,17 +188,22 @@
         rows_out = jnp.where(lane_out == me * frames + i, mean_row, rows_out)
         cols_out = jnp.where(lane_out == me * frames + i, mean_col, cols_out)
     for j in range(pieces):
-        outs[j][0] = rows_out[j * own : (j + 1) * own]
-        outs[j][1] = cols_out[j * own : (j + 1) * own]
+        for k, v in enumerate((rows_out, cols_out)):
+            piece_out = v[j * own : (j + 1) * own]
+            if j % 2:
+                odd_ref[j // 2, k] = piece_out
+            else:
+                evens[j // 2][k] = piece_out
 
 
 def fine_part(codes, tiles, own, window, region, payloads):
     pieces = len(payloads)
     return pl.pallas_call(
         functools.partial(fine_kernel, pieces, own, region),
-        out_shape=[jax.ShapeDtypeStruct((2, own, window), jnp.float32)] * pieces,
+        out_shape=[jax.ShapeDtypeStruct((2, own, window), jnp.float32)] * (pieces // 2)
+        + [jax.ShapeDtypeStruct((pieces // 2, 2, own, window), jnp.float32)],
         in_specs=[VMEM, VMEM] + [VMEM] * pieces,
-        out_specs=[VMEM] * pieces,
+        out_specs=[VMEM] * (pieces // 2 + 1),
         compiler_params=SMALL,
         name="fine_part",
     )(codes, tiles, *payloads)
@@ -338,7 +343,7 @@
     )(q, f, gate, *([prev] if half else []))
 
 
-def finish_kernel(pieces, heads, channels, stats_ref, *refs):
+def finish_kernel(pieces, heads, channels, stats_ref, met_ref, *refs):
     scale = math.log2(math.e) / math.sqrt(channels)
     ins, (coarse_ref, fine_ref) = refs[:pieces], refs[pieces:]
     me = lax.axis_index("frames")
@@ -377,13 +382,13 @@
             preferred_element_type=jnp.float32,
         ) * (4.0 / (heads * size))
     for k in range(2):
-        fine = ins[0][k]
-        for j in range(1, pieces):
-            fine = fine + ins[j][k]
+        fine = met_ref[0, k]
+        for piece in ins:
+            fine = fine + piece[k]
         fine_ref[k] = fine
 
 
-def finish(stats, pieces, heads, channels):
+def finish(stats, met, pieces, heads, channels):
     quarter = stats.shape[2]
     rows = stats.shape[1] * 128
     return pl.pallas_call(
@@ -392,11 +397,11 @@
             jax.ShapeDtypeStruct((2, quarter // 4, rows // heads), jnp.float32),
             jax.ShapeDtypeStruct(pieces[0].shape, jnp.float32),
         ],
-        in_specs=[VMEM] * (1 + len(pieces)),
+        in_specs=[VMEM] * (2 + len(pieces)),
         out_specs=[VMEM, VMEM],
         compiler_params=SMALL,
         name="finish",
-    )(stats, *pieces)
+    )(stats, met, *pieces)
 
 
 def body(coarse_query, coarse_feat, fine_query, fine_tiles, track_pos, tile_list, tile_valid):
@@ -412,15 +417,19 @@
 
     ranks = [sorted(range(blocks), key=lambda b: (abs(b - blocks // 2), b))]
     halves = coarse_query.reshape(2, tracks * heads // 2, channels)
-    mine, payload = prepare(blocks, halves, fine_query, jnp.transpose(track_pos, (0, 2, 1)))
+    mine, payload, ids, codes = prepare(
+        blocks, owners, halves, fine_query, jnp.transpose(track_pos, (0, 2, 1)), tile_list, tile_valid
+    )
     first = lax.all_to_all(
         mine, "blk", split_axis=0, concat_axis=0, tiled=True, axis_index_groups=ranks
     )
     payloads = [payload] + [swap(payload, j) for j in range(1, owners)]
-    tiles, codes = fetch(tile_list, tile_valid, fine_tiles, owners, own)
+    tiles = fetch(ids, fine_tiles, owners)
     fine = fine_part(codes, tiles, own, window, region, payloads)
-    gate = fine[0]
-    fine = [fine[0]] + [swap(fine[j], j) for j in range(1, owners)]
+    evens, odd = fine[:-1], fine[-1]
+    gate = evens[0]
+    met = swap(odd, 1)
+    far = [swap(evens[e] + met[e], 2 * e) for e in range(1, owners // 2)]
 
     cells = jnp.transpose(coarse_feat, (1, 0, 2))
     second = swap(first, 1)
@@ -429,7 +438,7 @@
     stats = lax.all_to_all(
         stats, "blk", split_axis=0, concat_axis=0, tiled=True, axis_index_groups=ranks
     )
-    coarse_pos, fine_offset = finish(stats, fine, heads, channels)
+    coarse_pos, fine_offset = finish(stats, met, [gate] + far, heads, channels)
     return coarse_pos, jnp.transpose(fine_offset, (0, 2, 1))
 
 

time: 70.4 us -> 70.2 us (level)
    all_to_all x1, waiting for transfers between devices: 0.01 us -> 0.95 us  [body(): lax.all_to_all(stats, 'blk', split_axis=0, concat_axis=0, tiled=True, axi...]
    ppermute x7 -> x6, waiting for transfers between devices: 3.17 us -> 2.54 us  [swap(): return lax.ppermute(x, 'frames', [(i, i ^ j) for i in range(owners)])]
    ppermute x7 -> x6, starting transfers between devices: 3.86 us -> 3.89 us  [swap(): return lax.ppermute(x, 'frames', [(i, i ^ j) for i in range(owners)])]
  transfers between devices with their start and end apart: 8 -> 7, of which waited for: 3 -> 3; matrix products, arithmetic and copies ran while one was open for 0% -> 0% of each run, Pallas kernels for 31% -> 35%
where the time goes in v6:
time: 70.2 us; the launch traced here: 69.8 us
  Pallas kernels  26.7 us (38%)
  starting transfers between devices  24.1 us (34%)
  blocking collectives  14.8 us (21%)
  waiting for transfers between devices  3.49 us (5%)
    pallas_call x2, Pallas kernels, coarse_half(): pl.pallas_call(functools.partial(coarse_kernel, half), out_shape=jax.Shap...  21.2 us
    all_to_all x1, starting transfers between devices, body(): lax.all_to_all(stats, 'blk', split_axis=0, concat_axis=0, tiled=True, axi...  20.2 us
    all_to_all x1, blocking collectives, body(): lax.all_to_all(mine, 'blk', split_axis=0, concat_axis=0, tiled=True, axis...  14.8 us
    ppermute x6, starting transfers between devices, swap(): return lax.ppermute(x, 'frames', [(i, i ^ j) for i in range(owners)])  3.89 us
    ppermute x6, waiting for transfers between devices, swap(): return lax.ppermute(x, 'frames', [(i, i ^ j) for i in range(owners)])  2.54 us
    pallas_call x1, Pallas kernels, fetch(): pl.pallas_call(functools.partial(fetch_kernel, pieces), out_shape=jax.Sha...  2.54 us
  transfers between devices with their start and end apart: 7, of which 3 were waited for; matrix products, arithmetic and copies ran while one was open for 0% of the time, Pallas kernels for 35%

profile of v6, /device:TPU:0, one launch (start us, length us, event | category | flops | bytes accessed | tf_op | source)
XLA Modules:
  0.0 69.8 jit_solution(794442978030257974)
XLA Ops:
  0.6 1.2 %prepare.1 = (bf16[8,64,256]{2,1,0:T(8,128)(2,1)S(1)}, f32[8,128]{1,0:T(8,128)S(1)}, s32[4,1,4,8]{3,2,1,0:T(4,128)S(1)}, f32[32,8]{1,0:T(8,128)S(1)}) custom-call(bf16[2,64,256]{2,1,0:T(8,128)(2,1)} %bitcast.10, bf16[2,128]{1,0:T(2,128)(2,1)} %query_ref.1, s32[2,2,16]{2,1,0:T(2,128)} %bitcast.11, s32[4,1,4,8]{3,2,1,0:T(4,128)} %list_ref.1, ...), custom_call_target="tpu_custom_call" | custom-call | tf_op jit(solution)/shard_map/prepare/pallas_call | solution.py:79
  1.9 14.8 %all_to_all.10.q_ref = bf16[8,64,256]{2,1,0:T(8,128)(2,1)S(1)} all-to-all(bf16[8,64,256]{2,1,0:T(8,128)(2,1)S(1)} %get-tuple-element.11), channel_id=1, replica_groups={{16,12,20,8,24,4,28,0},{17,13,21,9,25,5,29,1},{18,14,22,10,26,6,30,2},{..., dimensions={0} | all-to-all | bytes 524288 | tf_op jit(solution)/shard_map/all_to_all | solution.py:423
  16.6 0.0 collective-permute-start
  16.6 0.5 collective-permute-start.1
  17.1 1.5 %collective-permute-start.2 = (f32[8,128]{1,0:T(8,128)S(1)}, f32[8,128]{1,0:T(8,128)S(1)}, u32[]{:S(2)}, u32[]{:S(2)}) collective-permute-start(f32[8,128]{1,0:T(8,128)S(1)} %get-tuple-element.14.refs_0_), channel_id=1, source_target_pairs={{0,2},{1,3},{2,0},{3,1},{4,6},{5,7},{6,4},{7,5},{8,10},{9,11},{10,... | collective-permute-start | bytes 12296 | tf_op jit(solution)/shard_map/ppermute | solution.py:416
  18.6 0.0 collective-permute-start.3
  18.6 2.5 %fetch.1.tiles_ref = bf16[4,4,8,64,128]{4,3,2,1,0:T(8,128)(2,1)S(1)} custom-call(s32[4,1,4,8]{3,2,1,0:T(4,128)S(1)} %get-tuple-element.13.ids_ref, bf16[4,64,64,128]{3,2,1,0:T(8,128)(2,1)} %tiles_ref.1), custom_call_target="tpu_custom_call" | custom-call | tf_op jit(solution)/shard_map/fetch/pallas_call | solution.py:118
  21.2 0.0 copy-start
  21.2 0.0 collective-permute-done.1.refs_1_
  21.2 0.0 collective-permute-done.2.refs_2_
  21.2 0.4 collective-permute-done.3.refs_3_
  21.7 0.9 %fine_part.1 = (f32[2,2,16]{2,1,0:T(2,128)S(1)}, f32[2,2,16]{2,1,0:T(2,128)S(1)}, f32[2,2,2,16]{3,2,1,0:T(2,128)S(1)}) custom-call(f32[32,8]{1,0:T(8,128)S(1)} %get-tuple-element.12.codes_ref, bf16[4,4,8,64,128]{4,3,2,1,0:T(8,128)(2,1)S(1)} %fetch.1.tiles_ref, f32[8,128]{1,0:T(8,128)S(1)} %get-tuple-element.14.refs_0_, ...), custom_call_target="tpu_custom_call" | custom-call | tf_op jit(solution)/shard_map/fine_part/pallas_call | solution.py:201
  22.5 0.3 collective-permute-start.4
  22.9 0.0 copy-done
  22.9 18.4 %shard_map.86.rest_0_ = f32[8,1,16,128]{3,2,1,0:T(8,128)S(1)} custom-call(bf16[8,64,256]{2,1,0:T(8,128)(2,1)S(1)} %all_to_all.10.q_ref, bf16[1020,4,256]{2,1,0:T(4,128)(2,1)S(1)} %bitcast.8, f32[2,2,16]{2,1,0:T(2,128)S(1)} %get-tuple-element.15.gate_ref.refs_0_), custom_call_target="tpu_custom_call" | custom-call | tf_op jit(solution)/shard_map/pallas_call | solution.py:336
  41.2 0.0 collective-permute-done.q_ref
  41.2 2.8 %shard_map.87 = f32[8,1,16,128]{3,2,1,0:T(8,128)} custom-call(bf16[8,64,256]{2,1,0:T(8,128)(2,1)S(1)} %collective-permute-done.q_ref, bf16[1020,4,256]{2,1,0:T(4,128)(2,1)S(1)} %bitcast.9, f32[2,2,16]{2,1,0:T(2,128)S(1)} %get-tuple-element.15.gate_ref.refs_0_, f32[8,1,16,128]{3,2,1,0:T(8,128)S(1)} %shard_map.86.rest_0_), custom_call_target="tpu_custom_call" | custom-call | tf_op jit(solution)/shard_map/pallas_call | solution.py:336
  44.1 20.2 %all-to-all-start.1 = ((f32[8,1,16,128]{3,2,1,0:T(8,128)}), f32[8,1,16,128]{3,2,1,0:T(8,128)S(1)}, u32[]{:S(2)}, u32[]{:S(2)}) async-start(f32[8,1,16,128]{3,2,1,0:T(8,128)} %shard_map.87), calls=%async_computation.1 | async-start | bytes 131072 | tf_op jit(solution)/shard_map/all_to_all | solution.py:438
  64.3 0.0 collective-permute-done.4.met_ref
  64.3 1.6 %collective-permute-start.5 = (f32[2,2,16]{2,1,0:T(2,128)S(1)}, f32[2,2,16]{2,1,0:T(2,128)S(1)}, u32[]{:S(2)}, u32[]{:S(2)}) collective-permute-start(f32[2,2,16]{2,1,0:T(2,128)S(1)} %fusion), channel_id=1, source_target_pairs={{0,2},{1,3},{2,0},{3,1},{4,6},{5,7},{6,4},{7,5},{8,10},{9,11},{10,... | collective-permute-start | bytes 776 | tf_op jit(solution)/shard_map/ppermute | solution.py:416
  65.9 2.1 %collective-permute-done.5.refs_1_ = f32[2,2,16]{2,1,0:T(2,128)S(1)} collective-permute-done((f32[2,2,16]{2,1,0:T(2,128)S(1)}, f32[2,2,16]{2,1,0:T(2,128)S(1)}, u32[]{:S(2)}, u32[]{:S(2)}) %collective-permute-start.5) | collective-permute-done | bytes 288 | tf_op jit(solution)/shard_map/ppermute | solution.py:416
  68.0 0.9 %all-to-all-done.1.stats_ref = f32[8,1,16,128]{3,2,1,0:T(8,128)S(1)} async-done(((f32[8,1,16,128]{3,2,1,0:T(8,128)}), f32[8,1,16,128]{3,2,1,0:T(8,128)S(1)}, u32[]{:S(2)}, u32[]{:S(2)}) %all-to-all-start.1) | async-done | bytes 65568 | tf_op jit(solution)/shard_map/all_to_all | solution.py:438
  68.9 0.8 %finish.1 = (f32[2,4,8]{2,1,0:T(4,128)}, f32[2,2,16]{2,1,0:T(2,128)}) custom-call(f32[8,1,16,128]{3,2,1,0:T(8,128)S(1)} %all-to-all-done.1.stats_ref, f32[2,2,2,16]{3,2,1,0:T(2,128)S(1)} %collective-permute-done.4.met_ref, f32[2,2,16]{2,1,0:T(2,128)S(1)} %get-tuple-element.15.gate_ref.refs_0_, f32[2,2,16]{2,1,0:T(2,128)S(1)} %collective-permute-done.5.refs_1_), custom_call_target="tpu_custom_call" | custom-call | tf_op jit(solution)/shard_map/finish/pallas_call | solution.py:394
  (1 shorter events, 0.0 us)
Async XLA Ops:
  16.6 24.6 %collective-permute-start = (bf16[8,64,256]{2,1,0:T(8,128)(2,1)S(1)}, bf16[8,64,256]{2,1,0:T(8,128)(2,1)S(1)}, u32[]{:S(2)}, u32[]{:S(2)}) collective-permute-start(bf16[8,64,256]{2,1,0:T(8,128)(2,1)S(1)} %all_to_all.10.q_ref), channel_id=1, source_target_pairs={{0,1},{1,0},{2,3},{3,2},{4,5},{5,4},{6,7},{7,6},{8,9},{9,8},{10,11... | collective-permute-start | bytes 786440 | tf_op jit(solution)/shard_map/ppermute | solution.py:416
  16.6 4.6 %collective-permute-start.1 = (f32[8,128]{1,0:T(8,128)S(1)}, f32[8,128]{1,0:T(8,128)S(1)}, u32[]{:S(2)}, u32[]{:S(2)}) collective-permute-start(f32[8,128]{1,0:T(8,128)S(1)} %get-tuple-element.14.refs_0_), channel_id=1, source_target_pairs={{0,1},{1,0},{2,3},{3,2},{4,5},{5,4},{6,7},{7,6},{8,9},{9,8},{10,11... | collective-permute-start | bytes 12296 | tf_op jit(solution)/shard_map/ppermute | solution.py:416
  17.1 4.1 %collective-permute-start.2 = (f32[8,128]{1,0:T(8,128)S(1)}, f32[8,128]{1,0:T(8,128)S(1)}, u32[]{:S(2)}, u32[]{:S(2)}) collective-permute-start(f32[8,128]{1,0:T(8,128)S(1)} %get-tuple-element.14.refs_0_), channel_id=1, source_target_pairs={{0,2},{1,3},{2,0},{3,1},{4,6},{5,7},{6,4},{7,5},{8,10},{9,11},{10,... | collective-permute-start | bytes 12296 | tf_op jit(solution)/shard_map/ppermute | solution.py:416
  18.6 3.0 %collective-permute-start.3 = (f32[8,128]{1,0:T(8,128)S(1)}, f32[8,128]{1,0:T(8,128)S(1)}, u32[]{:S(2)}, u32[]{:S(2)}) collective-permute-start(f32[8,128]{1,0:T(8,128)S(1)} %get-tuple-element.14.refs_0_), channel_id=1, source_target_pairs={{0,3},{1,2},{2,1},{3,0},{4,7},{5,6},{6,5},{7,4},{8,11},{9,10},{10,... | collective-permute-start | bytes 12296 | tf_op jit(solution)/shard_map/ppermute | solution.py:416
  21.2 1.7 %copy-start = (bf16[4,1020,256]{2,0,1:T(4,128)(2,1)S(1)}, bf16[4,1020,256]{2,0,1:T(4,128)(2,1)}, u32[]{:S(2)}) copy-start(bf16[4,1020,256]{2,0,1:T(4,128)(2,1)} %param.8) | copy-start | bytes 6266884
  22.5 41.8 %collective-permute-start.4 = (f32[2,2,2,16]{3,2,1,0:T(2,128)S(1)}, f32[2,2,2,16]{3,2,1,0:T(2,128)S(1)}, u32[]{:S(2)}, u32[]{:S(2)}) collective-permute-start(f32[2,2,2,16]{3,2,1,0:T(2,128)S(1)} %get-tuple-element.16), channel_id=1, source_target_pairs={{0,1},{1,0},{2,3},{3,2},{4,5},{5,4},{6,7},{7,6},{8,9},{9,8},{10,11... | collective-permute-start | bytes 1544 | tf_op jit(solution)/shard_map/ppermute | solution.py:416
  44.1 24.8 %all-to-all-start.1 = ((f32[8,1,16,128]{3,2,1,0:T(8,128)}), f32[8,1,16,128]{3,2,1,0:T(8,128)S(1)}, u32[]{:S(2)}, u32[]{:S(2)}) async-start(f32[8,1,16,128]{3,2,1,0:T(8,128)} %shard_map.87), calls=%async_computation.1 | async-start | bytes 131072 | tf_op jit(solution)/shard_map/all_to_all | solution.py:438
  64.3 3.7 %collective-permute-start.5 = (f32[2,2,16]{2,1,0:T(2,128)S(1)}, f32[2,2,16]{2,1,0:T(2,128)S(1)}, u32[]{:S(2)}, u32[]{:S(2)}) collective-permute-start(f32[2,2,16]{2,1,0:T(2,128)S(1)} %fusion), channel_id=1, source_target_pairs={{0,2},{1,3},{2,0},{3,1},{4,6},{5,7},{6,4},{7,5},{8,10},{9,11},{10,... | collective-permute-start | bytes 776 | tf_op jit(solution)/shard_map/ppermute | solution.py:416
